TPU v7x, 512 devices: a whole 4x8x8 slice. The times are simulated.
512 devices in a mesh: rep: 32 (over z, x), tp: 16 (over y, core).
Axes of the slice: x: 4, y: 8, z: 8, core: 2. Of those that a mesh axis runs over, the one named last changes fastest.
Arguments:
- tokens: bfloat16 [16384, 8192], P('rep', 'tp'), may hold values from -6 to 6
- frozen_weight: bfloat16 [8192, 2048], P('tp'), may hold values from -0.0625 to 0.0625
- cotangent: bfloat16 [16384, 2048], P('rep', 'tp'), may hold values from -6 to 6
- adapter_input_maps: bfloat16 [32, 16, 8192], P('rep', None, 'tp'), may hold values from -0.0625 to 0.0625
- adapter_output_maps: bfloat16 [32, 16, 2048], P('rep', None, 'tp'), may hold values from -0.375 to 0.375
- tenant: int32 [128], P('rep'), may hold values from 0 to 31
- adapter_storage_slot: int32 [32], replicated, may hold values from 0 to 31, each once
Outputs:
- projected: float32 [16384, 2048], P('rep', 'tp')
- token_gradient: float32 [16384, 8192], P('rep', 'tp')
- adapter_input_gradient: float32 [32, 16, 8192], P('rep', None, 'tp')
- adapter_output_gradient: float32 [32, 16, 2048], P('rep', None, 'tp')
Inputs may be any that keep to these rules, and one draw needn't show every extreme that they name: `adapter_storage_slot`: each slot holds exactly one adapter.
All inputs are finite; a program needn't handle non-finite values.
Results may differ from a plain program's by a relative error of at most 0.00035.
Values may be sent and summed in bfloat16 or wider, within the bound.
A program may use at most 64 MiB of HBM per device.

v0:
```python
import jax
import jax.numpy as jnp
from jax import lax
from jax.sharding import PartitionSpec as P

HIGH_ACCURACY = lax.Precision.HIGHEST


def slot_lookup(tenants, adapter_storage_slot):
    labels = jnp.arange(adapter_storage_slot.shape[0], dtype=jnp.int32)
    return jnp.sum(
        jnp.where(tenants[:, None] == labels[None, :], adapter_storage_slot[None, :], 0), axis=1
    )


def shards(
    tokens,
    frozen_weight,
    cotangent,
    adapter_input_maps,
    adapter_output_maps,
    tenant,
    adapter_storage_slot,
):
    token_count = tokens.shape[0]
    blocks = tenant.shape[0]
    block_len = token_count // blocks
    tenant_token_count = adapter_input_maps.shape[0]
    inputs_all, outputs_all = (
        lax.all_gather(adapter_input_maps, "rep", axis=0, tiled=True),
        lax.all_gather(adapter_output_maps, "rep", axis=0, tiled=True),
    )
    adapter_list = inputs_all.shape[0]
    labels = jnp.arange(adapter_list, dtype=jnp.int32)
    block_storage_slot = slot_lookup(tenant, adapter_storage_slot)
    tenant_selector = (block_storage_slot[:, None] == labels[None, :]).astype(jnp.float32)
    picker = tenant_selector.astype(jnp.bfloat16)
    input_map_rows = jnp.einsum(
        "bs,srd->brd", picker, inputs_all, preferred_element_type=jnp.float32
    )
    output_map_rows = jnp.einsum(
        "bs,src->brc", picker, outputs_all, preferred_element_type=jnp.float32
    )
    token_rows = tokens.reshape(blocks, block_len, -1).astype(jnp.float32)
    grad_rows = cotangent.reshape(blocks, block_len, -1).astype(jnp.float32)
    part_in = jnp.einsum("bnd,brd->bnr", token_rows, input_map_rows, precision=HIGH_ACCURACY)
    part_back = jnp.einsum("bnc,brc->bnr", grad_rows, output_map_rows, precision=HIGH_ACCURACY)
    rank_in, rank_back = lax.psum((part_in, part_back), "tp")
    base_terms = jnp.dot(tokens, frozen_weight, preferred_element_type=jnp.float32)
    base = lax.psum_scatter(base_terms, "tp", scatter_dimension=1, tiled=True)
    low_rank = 2.0 * jnp.einsum("bnr,brc->bnc", rank_in, output_map_rows, precision=HIGH_ACCURACY)
    projected = base + low_rank.reshape(token_count, -1)
    through = lax.dot_general(
        lax.all_gather(cotangent, "tp", axis=1, tiled=True),
        frozen_weight,
        (((1,), (1,)), ((), ())),
        preferred_element_type=jnp.float32,
    )
    side = 2.0 * jnp.einsum("bnr,brd->bnd", rank_back, input_map_rows, precision=HIGH_ACCURACY)
    token_gradient = through + side.reshape(token_count, -1)
    input_map_gradient = 2.0 * jnp.einsum(
        "bnr,bnd->brd", rank_back, token_rows, precision=HIGH_ACCURACY
    )
    output_map_gradient = 2.0 * jnp.einsum(
        "bnr,bnc->brc", rank_in, grad_rows, precision=HIGH_ACCURACY
    )
    every_tenant = lax.all_gather(tenant, "rep", axis=0, tiled=True)
    every_slot = slot_lookup(every_tenant, adapter_storage_slot)
    owned = lax.axis_index("rep") * tenant_token_count + jnp.arange(
        tenant_token_count, dtype=jnp.int32
    )
    owner_select = (every_slot[:, None] == owned[None, :]).astype(jnp.float32)
    counts = block_len * jnp.sum(owner_select, axis=0)
    adapter_scale = 1.0 / jnp.maximum(counts, 1.0)
    table_in = jnp.einsum(
        "ol,oht->lht", tenant_selector, input_map_gradient, precision=HIGH_ACCURACY
    )
    table_out = jnp.einsum(
        "pa,pne->ane", tenant_selector, output_map_gradient, precision=HIGH_ACCURACY
    )
    input_gradient_sum, output_gradient_sum = (
        lax.psum_scatter(table_in, "rep", scatter_dimension=0, tiled=True),
        lax.psum_scatter(table_out, "rep", scatter_dimension=0, tiled=True),
    )
    adapter_input_gradient = input_gradient_sum * adapter_scale[:, None, None]
    adapter_output_gradient = output_gradient_sum * adapter_scale[:, None, None]
    return (projected, token_gradient, adapter_input_gradient, adapter_output_gradient)


def solution(mesh):
    placed = (
        P("rep", "tp"),
        P("tp", None),
        P("rep", "tp"),
        P("rep", None, "tp"),
        P("rep", None, "tp"),
        P("rep"),
        P(),
    )
    return jax.shard_map(
        shards,
        mesh=mesh,
        in_specs=placed,
        out_specs=(P("rep", "tp"), P("rep", "tp"), P("rep", None, "tp"), P("rep", None, "tp")),
        check_vma=False,
    )
```

profile of v0, /device:TPU:1, one launch (start us, length us, event | category | flops | bytes accessed | tf_op | source)
XLA Modules:
  0.0 781.7 jit_solution(3900021885987403363)
XLA Ops:
  7.2 44.5 %all_gather.12 = bf16[32,16,512]{2,1,0:T(8,128)(2,1)S(1)} all-gather(bf16[1,16,512]{2,1,0:T(8,128)(2,1)} %param.10), channel_id=1, replica_groups=mesh['rep'=32,'tp'=16] {'rep'}, dimensions={0}, use_global_device_ids=true | all-gather | bytes 540672 | tf_op jit(solution)/shard_map/all_gather | solution.py:30
  51.7 32.8 %all_gather.13 = bf16[32,16,128]{2,1,0:T(8,128)(2,1)S(1)} all-gather(bf16[1,16,128]{2,1,0:T(8,128)(2,1)} %param.11), channel_id=1, replica_groups=mesh['rep'=32,'tp'=16] {'rep'}, dimensions={0}, use_global_device_ids=true | all-gather | bytes 135168 | tf_op jit(solution)/shard_map/all_gather | solution.py:31
  84.6 0.9 select_reduce_fusion.1
  86.0 2.2 convolution_bitcast_fusion.1
  88.2 0.9 convolution_bitcast_fusion
  89.2 124.5 %all-reduce.4.cloned.1.call-done = (f32[4,128,16]{1,2,0:T(8,128)}, f32[4,128,16]{1,2,0:T(8,128)}) async-done(((f32[4,128,16]{1,2,0:T(8,128)}, f32[4,128,16]{1,2,0:T(8,128)}), (f32[4,128,16]{1,2,0:T(8,128)}, f32[4,128,16]{1,2,0:T(8,128)})) %all-reduce.4.cloned.1.call-update) | async-done | bytes 65552 | tf_op jit(solution)/shard_map/psum | solution.py:48
  213.7 1.0 convolution_multiply_fusion.3
  215.1 0.9 copy.36
  216.0 1.1 convolution_multiply_fusion.2
  217.1 0.7 fusion.2
  217.8 1.6 copy.34
  220.1 3.2 fusion.23
  223.3 1.3 dynamic-slice
  225.5 17.2 %all-reduce = s32[128]{0:T(128)S(1)} all-reduce(s32[128]{0:T(128)S(1)} %dynamic-update-slice), channel_id=1, replica_groups=mesh['rep'=32,'tp'=16] {'rep'}, use_global_device_ids=true, to_apply=%add | all-reduce | flops 128 | bytes 1024
  242.8 0.6 fusion.22
  244.7 2.0 convolution_multiply_fusion
  246.7 187.2 %reduce-scatter.8.cloned.1.call-done = f32[1,16,128]{2,1,0:T(8,128)} async-done(((f32[32,16,128]{2,1,0:T(8,128)}), f32[1,16,128]{2,1,0:T(8,128)}) %reduce-scatter.8.cloned.1.call-update) | async-done | bytes 8208 | tf_op jit(solution)/shard_map/reduce_scatter | solution.py:83
  434.0 1.3 broadcast_multiply_fusion.1
  435.3 224.1 %reduce-scatter.6.cloned.1.call-done = f32[1,16,512]{2,1,0:T(8,128)} async-done(((f32[32,16,512]{2,1,0:T(8,128)}), f32[1,16,512]{2,1,0:T(8,128)}) %reduce-scatter.6.cloned.1.call-update) | async-done | bytes 32784 | tf_op jit(solution)/shard_map/reduce_scatter | solution.py:82
  659.4 1.4 broadcast_multiply_fusion
  660.8 47.3 %all-gather.2.cloned.1.call-done = bf16[512,2048]{1,0:T(8,128)(2,1)} async-done(((bf16[512,128]{1,0:T(8,128)(2,1)}), bf16[512,2048]{1,0:T(8,128)(2,1)}) %all-gather.2.cloned.1.call-update) | async-done | bytes 2097168 | tf_op jit(solution)/shard_map/all_gather | solution.py:54
  708.1 4.1 convolution_add_fusion
  712.2 61.4 %reduce-scatter.4.cloned.1.call-done = f32[512,128]{1,0:T(8,128)} async-done(((f32[512,2048]{1,0:T(8,128)}), f32[512,128]{1,0:T(8,128)}) %reduce-scatter.4.cloned.1.call-update) | async-done | bytes 262160 | tf_op jit(solution)/shard_map/reduce_scatter | solution.py:50
  773.5 1.7 bitcast_add_fusion
  (31 shorter events, 2.8 us)
Async XLA Ops:
  7.2 212.9 %copy-start = (bf16[512,2048]{1,0:T(8,128)(2,1)S(1)}, bf16[512,2048]{1,0:T(8,128)(2,1)}, u32[]{:S(2)}) copy-start(bf16[512,2048]{1,0:T(8,128)(2,1)} %param.8) | copy-start | bytes 6291460
  7.2 208.8 %copy-start.1 = (bf16[512,512]{1,0:T(8,128)(2,1)S(1)}, bf16[512,512]{1,0:T(8,128)(2,1)}, u32[]{:S(2)}) copy-start(bf16[512,512]{1,0:T(8,128)(2,1)} %param.7) | copy-start | bytes 1572868
  7.2 81.0 %copy-start.2 = (bf16[512,128]{1,0:T(8,128)(2,1)S(1)}, bf16[512,128]{1,0:T(8,128)(2,1)}, u32[]{:S(2)}) copy-start(bf16[512,128]{1,0:T(8,128)(2,1)} %param.9) | copy-start | bytes 393220
  7.2 206.5 %all-reduce.4.cloned.1.call-start = ((), (), s32[]{:S(2)}) async-start(), calls=%async_computation.7 | async-start | bytes 131072 | tf_op jit(solution)/shard_map/psum | solution.py:48
  89.2 344.8 %reduce-scatter.8.cloned.1.call-start = ((), (), s32[]{:S(2)}) async-start(), calls=%async_computation.6 | async-start | bytes 270336 | tf_op jit(solution)/shard_map/reduce_scatter | solution.py:83
  215.9 443.5 %reduce-scatter.6.cloned.1.call-start = ((), (), s32[]{:S(2)}) async-start(), calls=%async_computation.5 | async-start | bytes 1081344 | tf_op jit(solution)/shard_map/reduce_scatter | solution.py:82
  219.4 488.6 %all-gather.2.cloned.1.call-start = ((), (), s32[]{:S(2)}) async-start(), calls=%async_computation.4 | async-start | bytes 2228224 | tf_op jit(solution)/shard_map/all_gather | solution.py:54
  220.0 553.5 %reduce-scatter.4.cloned.1.call-start = ((), (), s32[]{:S(2)}) async-start(), calls=%async_computation.3 | async-start | bytes 4456448 | tf_op jit(solution)/shard_map/reduce_scatter | solution.py:50
  223.3 2.0 copy-start.5
  223.3 19.5 %copy-start.6 = (s32[32]{0:T(128)S(1)}, s32[32]{0:T(128)}, u32[]{:S(2)}) copy-start(s32[32]{0:T(128)} %param.13) | copy-start | bytes 388
  223.3 20.8 %copy-start.3 = (f32[4,128,16]{1,2,0:T(8,128)S(1)}, f32[4,128,16]{1,2,0:T(8,128)}, u32[]{:S(2)}) copy-start(f32[4,128,16]{1,2,0:T(8,128)} %get-tuple-element.8) | copy-start | bytes 98308
  223.3 21.5 %copy-start.4 = (f32[4,128,16]{1,2,0:T(8,128)S(1)}, f32[4,128,16]{1,2,0:T(8,128)}, u32[]{:S(2)}) copy-start(f32[4,128,16]{1,2,0:T(8,128)} %get-tuple-element.9) | copy-start | bytes 98308
Sparse Core Ops, SparseCore 0:
  89.3 124.3 all-reduce.3
  218.6 215.2 reduce-scatter.7
  438.4 220.9 reduce-scatter.5
  661.3 46.7 all-gather.1
  710.8 62.7 reduce-scatter.3
where the time goes:
time: 784 us; the launch traced here: 782 us
  waiting for transfers between devices  645 us (82%)
  blocking collectives  94.6 us (12%)
  matrix products  16.8 us (2%)
  between operations  15.2 us (2%)
    reduce_scatter x1, waiting for transfers between devices, shards(): lax.psum_scatter(table_in, 'rep', scatter_dimension=0, tiled=True)  224 us
    reduce_scatter x1, waiting for transfers between devices, shards(): lax.psum_scatter(table_out, 'rep', scatter_dimension=0, tiled=True)  187 us
    psum x1, waiting for transfers between devices, shards(): rank_in, rank_back = lax.psum((part_in, part_back), 'tp')  124 us
    reduce_scatter x1, waiting for transfers between devices, shards(): base = lax.psum_scatter(base_terms, 'tp', scatter_dimension=1, tiled=True)  61.4 us
    all_gather x1, waiting for transfers between devices, shards(): lax.all_gather(cotangent, 'tp', axis=1, tiled=True)  47.3 us
    all_gather x1, blocking collectives, shards(): lax.all_gather(adapter_input_maps, 'rep', axis=0, tiled=True)  44.5 us
    all_gather x1, blocking collectives, shards(): lax.all_gather(adapter_output_maps, 'rep', axis=0, tiled=True)  32.8 us
    unnamed x1, blocking collectives  17.2 us
  transfers between devices with their start and end apart: 5, of which 5 were waited for; matrix products, arithmetic and copies ran while one was open for 2% of the time, Pallas kernels for 0%

commit v1 on v0

v1 whole, which is shorter than its diff:
```python
import functools

import jax
import jax.numpy as jnp
from jax import lax
from jax.experimental import pallas as pl
from jax.experimental.pallas import tpu as pltpu
from jax.sharding import PartitionSpec as P

MESH = pl.DeviceIdType.MESH
F32, BF16 = jnp.float32, jnp.bfloat16
NX, NY, NZ, NC = 4, 8, 8, 2
NT = NY * NC
BLOCK = 128
NT_DIMS = (((1,), (1,)), ((), ()))
TN_DIMS = (((0,), (0,)), ((), ()))


def dot(a, b):
    return jnp.dot(a, b, preferred_element_type=F32)


def dot_nt(a, b):
    return lax.dot_general(a, b, NT_DIMS, preferred_element_type=F32)


def dot_tn(a, b):
    return lax.dot_general(a, b, TN_DIMS, preferred_element_type=F32)


def two_parts(v):
    high = v.astype(BF16)
    low = (v - high.astype(F32)).astype(BF16)
    return jnp.concatenate([high, low], axis=0)


def kernel(
    tenant, storage, tok, w, cot, ain, aout,
    proj, tgrad, gin, gout,
    maps, sel, cnt, cotf, tokp, wp, base, rs_right, rs_left,
    part, part_in, full, gx, gz_out, gz_in,
    ssem, rsem, lsem,
):
    r, t = lax.axis_index("rep"), lax.axis_index("tp")
    z, x = lax.div(r, NX), lax.rem(r, NX)
    y, c = lax.div(t, NC), lax.rem(t, NC)
    rows = tok.shape[0]
    half = rows // 2
    nb = rows // BLOCK
    feat = tok.shape[1]
    rank = ain.shape[1]
    grouped = feat + cot.shape[1]
    other = 1 - c

    def at_y(d):
        return (r, lax.rem(y + d + NY, NY) * NC + c)

    def at_x(d):
        return (z * NX + lax.rem(x + d + NX, NX), t)

    def at_z(d):
        return (lax.rem(z + d + NZ, NZ) * NX + x, t)

    mate = (r, y * NC + other)
    counter = [0]
    sent = []

    def copy_to(src, dst, device):
        i = counter[0]
        counter[0] += 1
        made = pltpu.make_async_remote_copy(
            src_ref=src, dst_ref=dst, send_sem=ssem.at[i], recv_sem=rsem.at[i],
            device_id=device, device_id_type=MESH,
        )
        made.start()
        sent.append(made)
        return made

    local = [
        pltpu.make_async_copy(ain.at[0], maps.at[r, :, pl.ds(0, feat)], lsem.at[0]),
        pltpu.make_async_copy(aout.at[0], maps.at[r, :, pl.ds(feat, grouped - feat)], lsem.at[1]),
        pltpu.make_async_copy(cot, cotf.at[y, :, pl.ds(pl.multiple_of(c * 128, 128), 128)], lsem.at[2]),
    ]
    for made in local:
        made.start()
    lane = lax.broadcasted_iota(jnp.int32, (1, 128), 1)
    slots = [storage[tenant[b]] for b in range(nb)]
    for b in range(nb):
        sel[0, b:b + 1, :] = jnp.where(lane == slots[b], 1.0, 0.0).astype(F32)

    barrier = pltpu.get_barrier_semaphore()
    greeted = [mate, at_y(1), at_y(-1), at_x(1), at_x(2), at_x(3), at_z(1), at_z(-1)]
    for device in greeted:
        pl.semaphore_signal(barrier, inc=1, device_id=device, device_id_type=MESH)
    pl.semaphore_wait(barrier, len(greeted))
    for made in local:
        made.wait()

    maps_x = [copy_to(maps.at[r], maps.at[r], at_x(k)) for k in (1, 2, 3)]
    sel_x = [copy_to(sel.at[0], sel.at[k], at_x(k)) for k in (1, 2, 3)]

    def cot_at(yy, cc, lo, size):
        return cotf.at[yy, pl.ds(lo, size), pl.ds(pl.multiple_of(cc * 128, 128), 128)]

    ag_right, ag_left, ag_mate = {}, {}, []
    ag_right[1] = copy_to(cot, cot_at(y, c, 0, rows), at_y(1))
    ag_left[1] = copy_to(cot, cot_at(y, c, 0, rows), at_y(-1))
    tok_mate = copy_to(tok, tokp, mate)
    order = (4, 3, 5, 2, 6, 1, 7, 0)
    w_mate = {}

    def w_cols(d, cc):
        yy = lax.rem(y + d, NY)
        return pl.ds(pl.multiple_of(yy * (NC * 128) + cc * 128, 128), 128)

    for d in order:
        w_mate[d] = copy_to(w.at[:, w_cols(d, other)], wp.at[d], mate)
    ag_mate.append(copy_to(cot, cot_at(y, c, 0, rows), mate))

    for d in order:
        base[d] = dot(tok[...], w[:, w_cols(d, c)])

    for made in maps_x:
        made.wait_recv()
    mz_right, mz_left = {}, {}

    def maps_at(zz, lo, size):
        return maps.at[pl.ds(lax.rem(zz + NZ, NZ) * NX + lo, size)]

    mz_right[1] = copy_to(maps_at(z, 0, NX), maps_at(z, 0, NX), at_z(1))
    mz_left[1] = copy_to(maps_at(z, 0, NX), maps_at(z, 0, NX), at_z(-1))

    def ag_step(s):
        ag_right[s].wait_recv()
        ag_left[s].wait_recv()
        lo_y, hi_y = lax.rem(y - s + NY, NY), lax.rem(y + s, NY)
        size = rows if s < 3 else half
        piece = cot_at(lo_y, c, 0, size)
        ag_right[s + 1] = copy_to(piece, piece, at_y(1))
        piece = cot_at(hi_y, c, rows - size, size)
        ag_left[s + 1] = copy_to(piece, piece, at_y(-1))
        for yy in (lo_y, hi_y):
            piece = cot_at(yy, c, 0, rows)
            ag_mate.append(copy_to(piece, piece, mate))

    def mz_step(s):
        mz_right[s].wait_recv()
        mz_left[s].wait_recv()
        size = NX if s < 3 else NX // 2
        piece = maps_at(z - s, 0, size)
        mz_right[s + 1] = copy_to(piece, piece, at_z(1))
        piece = maps_at(z + s, NX - size, size)
        mz_left[s + 1] = copy_to(piece, piece, at_z(-1))

    rs = {}

    def rs_rows(h):
        return pl.ds(0 if h == "A" else half, half)

    def rs_send(way, h, d):
        slot = len([k for k in rs if k[0] == way])
        target = rs_right if way > 0 else rs_left
        made = copy_to(base.at[(way * d) % NY, rs_rows(h)], target.at[slot], at_y(way))
        rs[way, h, d] = (made, slot)

    def rs_take(way, h, d):
        made, slot = rs[way, h, d]
        made.wait_recv()
        source = rs_right if way > 0 else rs_left
        base[(way * (d - 1)) % NY, rs_rows(h)] += source[slot]

    def rs_hop(d, first):
        right, left = ("A", "B") if first else ("B", "A")
        rs_take(1, right, d + 1)
        rs_send(1, right, d)
        rs_take(-1, left, d + 1)
        rs_send(-1, left, d)

    def add_mate(d):
        w_mate[d].wait_recv()
        base[d] += dot(tokp[...], wp[d])

    ag_step(1)
    tok_mate.wait_recv()
    add_mate(4)
    rs_send(1, "A", 4)
    rs_send(-1, "B", 4)
    add_mate(3)
    rs_send(1, "B", 3)
    add_mate(5)
    rs_send(-1, "A", 3)
    mz_step(1)
    ag_step(2)
    add_mate(2)
    add_mate(6)
    mz_step(2)
    rs_hop(3, True)
    ag_step(3)
    for d in (1, 7, 0):
        add_mate(d)
    rs_hop(2, False)
    mz_step(3)

    ag_mate[0].wait_recv()
    tgrad[...] = dot_nt(cotf[y], w[:, pl.ds(pl.multiple_of(y * 256, 256), 256)])

    def through(yy):
        tgrad[...] += dot_nt(cotf[yy], w[:, pl.ds(pl.multiple_of(yy * 256, 256), 256)])

    ag_right[4].wait_recv()
    ag_left[4].wait_recv()
    far = cot_at(lax.rem(y + 4, NY), c, 0, rows)
    ag_mate.append(copy_to(far, far, mate))

    mz_right[4].wait_recv()
    mz_left[4].wait_recv()

    chosen = [maps[slots[b]] for b in range(nb)]
    for b in range(nb):
        here = pl.ds(b * BLOCK, BLOCK)
        pin = dot_nt(chosen[b][:, :feat], tok[here, :])
        pback = dot_nt(chosen[b][:, feat:], cot[here, :])
        part[b] = pin[:8]
        part[nb + b] = pin[8:]
        part[2 * nb + b] = pback[:8]
        part[3 * nb + b] = pback[8:]
    sums = []
    for k in range(1, NT):
        tt = lax.rem(t + k, NT)
        sums.append(copy_to(part.at[tt], part_in.at[k], (r, tt)))

    for made in sel_x:
        made.wait_recv()
    cnt[0] = jnp.sum(jnp.sum(sel[...], axis=0), axis=0, keepdims=True)
    counted = [copy_to(cnt.at[0], cnt.at[k], at_z(k)) for k in range(1, NZ)]

    rs_hop(2, True)

    total = part[t]
    for made in sums:
        made.wait_recv()
    for k in range(1, NT):
        total = total + part_in[k]
    full[t] = total
    spread = [copy_to(full.at[t], full.at[t], (r, lax.rem(t + k, NT))) for k in range(1, NT)]

    rs_hop(1, False)
    for i, s in ((1, 1), (2, -1)):
        ag_mate[i].wait_recv()
        through(lax.rem(y - s + NY, NY))

    for made in spread:
        made.wait_recv()
    rin = [two_parts(jnp.concatenate([full[b], full[nb + b]], axis=0)) for b in range(nb)]
    rback = [two_parts(jnp.concatenate([full[2 * nb + b], full[3 * nb + b]], axis=0)) for b in range(nb)]
    for b in range(nb):
        here = pl.ds(b * BLOCK, BLOCK)
        da = dot(rback[b], tok[here, :])
        db = dot(rin[b], cot[here, :])
        gx[0, b, :, :feat] = da[:rank] + da[rank:]
        gx[0, b, :, feat:] = db[:rank] + db[rank:]
    grads_x = [copy_to(gx.at[0], gx.at[k], at_x(k)) for k in (1, 2, 3)]

    rs_hop(1, True)
    for b in range(nb):
        here = pl.ds(b * BLOCK, BLOCK)
        amap = jnp.concatenate([chosen[b][:, :feat]] * 2, axis=0)
        bmap = jnp.concatenate([chosen[b][:, feat:]] * 2, axis=0)
        tgrad[here, :] += 2.0 * dot_tn(rback[b], amap)
        base[0, here, :] += 2.0 * dot_tn(rin[b], bmap)
    for i, s in ((3, 2), (4, -2)):
        ag_mate[i].wait_recv()
        through(lax.rem(y - s + NY, NY))

    for made in grads_x:
        made.wait_recv()
    grads_z = []
    for d in (4, 3, 5, 2, 6, 1, 7, 0):
        owner = lax.rem(z + d, NZ) * NX + x
        acc = jnp.zeros((rank, grouped), F32)
        for k in range(NX):
            weight = jnp.sum(jnp.where(lane == owner, sel[k], 0.0), axis=1, keepdims=True)
            for b in range(nb):
                acc = acc + weight[b:b + 1, :] * gx[k, b]
        gz_out[d] = acc
        if d:
            grads_z.append(copy_to(gz_out.at[d], gz_in.at[d], at_z(d)))

    for i, s in ((5, 3), (6, -3), (7, 4)):
        ag_mate[i].wait_recv()
        through(lax.rem(y - s + NY, NY))

    for way, first, second in ((1, "B", "A"), (-1, "A", "B")):
        rs_take(way, first, 1)
    for way, second in ((1, "A"), (-1, "B")):
        rs_take(way, second, 1)
    proj[...] = base[0]

    for made in counted:
        made.wait_recv()
    blocks_of = jnp.sum(cnt[...], axis=0)
    mine = jnp.sum(jnp.where(lane == r, blocks_of, 0.0), axis=1, keepdims=True)
    scale = 2.0 / jnp.maximum(mine * float(BLOCK), 1.0)
    for made in grads_z:
        made.wait_recv()
    acc = gz_out[0]
    for d in range(1, NZ):
        acc = acc + gz_in[d]
    acc = acc * scale
    gin[0] = acc[:, :feat]
    gout[0] = acc[:, feat:]
    for made in sent:
        made.wait_send()


COPIES = 128


def shards(tok, w, cot, ain, aout, tenant, storage):
    rows, feat = tok.shape
    cols = cot.shape[1]
    rank = ain.shape[1]
    nb = tenant.shape[0]
    grouped = feat + cols
    vmem = pl.BlockSpec(memory_space=pltpu.VMEM)
    smem = pl.BlockSpec(memory_space=pltpu.SMEM)
    return pl.pallas_call(
        kernel,
        out_shape=(
            jax.ShapeDtypeStruct((rows, cols), F32),
            jax.ShapeDtypeStruct((rows, feat), F32),
            jax.ShapeDtypeStruct(ain.shape, F32),
            jax.ShapeDtypeStruct(aout.shape, F32),
        ),
        in_specs=[smem, smem] + [vmem] * 5,
        out_specs=[vmem] * 4,
        scratch_shapes=[
            pltpu.VMEM((NX * NZ, rank, grouped), BF16),
            pltpu.VMEM((NX, nb, 128), F32),
            pltpu.VMEM((NZ, 1, 128), F32),
            pltpu.VMEM((NY, rows, NC * cols), BF16),
            pltpu.VMEM((rows, feat), BF16),
            pltpu.VMEM((NY, feat, cols), BF16),
            pltpu.VMEM((NY, rows, cols), F32),
            pltpu.VMEM((7, rows // 2, cols), F32),
            pltpu.VMEM((7, rows // 2, cols), F32),
            pltpu.VMEM((NT, 8, 128), F32),
            pltpu.VMEM((NT, 8, 128), F32),
            pltpu.VMEM((NT, 8, 128), F32),
            pltpu.VMEM((NX, nb, rank, grouped), F32),
            pltpu.VMEM((NZ, rank, grouped), F32),
            pltpu.VMEM((NZ, rank, grouped), F32),
            pltpu.SemaphoreType.DMA((COPIES,)),
            pltpu.SemaphoreType.DMA((COPIES,)),
            pltpu.SemaphoreType.DMA((3,)),
        ],
        compiler_params=pltpu.CompilerParams(
            collective_id=0, has_side_effects=True, vmem_limit_bytes=56 * 1024 * 1024
        ),
    )(tenant, storage, tok, w, cot, ain, aout)


def solution(mesh):
    placed = (
        P("rep", "tp"),
        P("tp", None),
        P("rep", "tp"),
        P("rep", None, "tp"),
        P("rep", None, "tp"),
        P("rep"),
        P(),
    )
    return jax.shard_map(
        shards,
        mesh=mesh,
        in_specs=placed,
        out_specs=(P("rep", "tp"), P("rep", "tp"), P("rep", None, "tp"), P("rep", None, "tp")),
        check_vma=False,
    )
```

time: 784 us -> 78.4 us (0.10)
  waiting for transfers between devices: 645 us -> 0 us
  blocking collectives: 94.6 us -> 0 us
  Pallas kernels: 0 us -> 72.4 us
  matrix products: 16.8 us -> 0 us
  between operations: 15.2 us -> 0.66 us
    reduce_scatter x3 -> x0, waiting for transfers between devices: 473 us -> none  [the longest x1 224 us: shards(): lax.psum_scatter(table_in, 'rep', scatter_dimension=0, tiled=True)]
    psum x1 -> x0, waiting for transfers between devices: 124 us -> none  [shards(): rank_in, rank_back = lax.psum((part_in, part_back), 'tp')]
    all_gather x2 -> x0, blocking collectives: 77.3 us -> none  [the longest x1 44.5 us: shards(): lax.all_gather(adapter_input_maps, 'rep', axis=0, tiled=True)]
    pallas_call x0 -> x1, Pallas kernels: none -> 72.4 us  [shards(): pl.pallas_call(kernel, out_shape=(jax.ShapeDtypeStruct((rows, cols), F32)...]
    all_gather x1 -> x0, waiting for transfers between devices: 47.3 us -> none  [shards(): lax.all_gather(cotangent, 'tp', axis=1, tiled=True)]
    unnamed x1 -> x0, blocking collectives: 17.2 us -> none
    dot_general x12 -> x0, matrix products: 16.8 us -> none  [the longest x1 4.11 us: shards(): lax.dot_general(lax.all_gather(cotangent, 'tp', axis=1, tiled=True), froz...]
  transfers between devices with their start and end apart: 5 -> 0, of which waited for: 5 -> 0; matrix products, arithmetic and copies ran while one was open for 2% -> 0% of each run, Pallas kernels for 0% -> 0%
where the time goes in v1:
time: 78.4 us; the launch traced here: 78.2 us
  Pallas kernels  72.4 us (92%)
  local copies, waits for them, and re-layouts  5.16 us (7%)
    pallas_call x1, Pallas kernels, shards(): pl.pallas_call(kernel, out_shape=(jax.ShapeDtypeStruct((rows, cols), F32)...  72.4 us
    unnamed x8, local copies, waits for them, and re-layouts  5.16 us

profile of v1, /device:TPU:1, one launch (start us, length us, event | category | flops | bytes accessed | tf_op | source)
XLA Modules:
  0.0 78.2 jit_solution(17981402825332406679)
XLA Ops:
  0.6 72.4 %shard_map.102 = (f32[512,128]{1,0:T(8,128)}, f32[512,512]{1,0:T(8,128)}, f32[1,16,512]{2,1,0:T(8,128)}, f32[1,16,128]{2,1,0:T(8,128)}) custom-call(s32[4]{0:T(128)} %tenant.1, s32[32]{0:T(128)} %storage.1, bf16[512,512]{1,0:T(8,128)(2,1)} %tok.1, bf16[512,2048]{1,0:T(8,128)(2,1)} %w.1, bf16[512,128]{1,0:T(8,128)(2,1)} %cot.1, bf16[1,16,512]{2,1,0:T(8,128)(2,1)} %ain.1, ...), custom_call_target="tpu_custom_call" | custom-call | tf_op jit(solution)/shard_map/pallas_call | solution.py:327
  73.1 0.0 copy-start
  73.1 0.0 copy-start.1
  73.1 1.7 %copy.15 = f32[512,128]{1,0:T(8,128)} copy(f32[512,128]{1,0:T(8,128)} %get-tuple-element.8) | data formatting | bytes 524288
  74.8 2.3 %copy.16 = f32[512,512]{1,0:T(8,128)} copy(f32[512,512]{1,0:T(8,128)} %get-tuple-element.9) | data formatting | bytes 2097152
  77.0 0.0 copy-done
  77.0 0.6 copy.17
  77.6 0.0 copy-done.1
  77.6 0.6 copy.18
Async XLA Ops:
  73.1 4.0 %copy-start = (f32[1,16,512]{2,1,0:T(8,128)S(1)}, f32[1,16,512]{2,1,0:T(8,128)}, u32[]{:S(2)}) copy-start(f32[1,16,512]{2,1,0:T(8,128)} %get-tuple-element.10) | copy-start | bytes 98308
  73.1 4.6 %copy-start.1 = (f32[1,16,128]{2,1,0:T(8,128)S(1)}, f32[1,16,128]{2,1,0:T(8,128)}, u32[]{:S(2)}) copy-start(f32[1,16,128]{2,1,0:T(8,128)} %get-tuple-element.11) | copy-start | bytes 24580

commit v2 on v1

v2 whole, which is shorter than its diff:
```python
import functools

import jax
import jax.numpy as jnp
from jax import lax
from jax.experimental import pallas as pl
from jax.experimental.pallas import tpu as pltpu
from jax.sharding import PartitionSpec as P

MESH = pl.DeviceIdType.MESH
F32, BF16 = jnp.float32, jnp.bfloat16
NX, NY, NZ, NC = 4, 8, 8, 2
NT = NY * NC
BLOCK = 128
NT_DIMS = (((1,), (1,)), ((), ()))
TN_DIMS = (((0,), (0,)), ((), ()))


def dot(a, b):
    return jnp.dot(a, b, preferred_element_type=F32)


def dot_nt(a, b):
    return lax.dot_general(a, b, NT_DIMS, preferred_element_type=F32)


def dot_tn(a, b):
    return lax.dot_general(a, b, TN_DIMS, preferred_element_type=F32)


def two_parts(v):
    high = v.astype(BF16)
    low = (v - high.astype(F32)).astype(BF16)
    return jnp.concatenate([high, low], axis=0)


def encode(v):
    top = jnp.max(jnp.max(jnp.abs(v), axis=0, keepdims=True), axis=1, keepdims=True)
    e = jnp.floor(jnp.log2(jnp.maximum(top, 1e-30)))
    scale = jnp.exp2(6.0 - e).astype(BF16).astype(F32)
    inverse = jnp.exp2(e - 6.0).astype(BF16).astype(F32)
    u = v * scale
    p = u * u
    p = p * p
    p = p * p
    p = p * p
    return jnp.where(u < 0, -p, p).astype(BF16), inverse


def decode(code, inverse):
    y = code.astype(F32)
    p = lax.rsqrt(lax.rsqrt(lax.rsqrt(lax.rsqrt(jnp.abs(y)))))
    return jnp.where(y < 0, -p, p) * inverse


def encode_grads(v, feat):
    left, linv = encode(v[:, :feat])
    right, rinv = encode(v[:, feat:])
    rank = v.shape[0]
    tail = jnp.concatenate(
        [jnp.broadcast_to(linv, (rank, 64)), jnp.broadcast_to(rinv, (rank, 64))], axis=1
    )
    return jnp.concatenate([left, right, tail.astype(BF16)], axis=1)


def decode_grads(m, feat):
    grouped = m.shape[1] - 128
    linv = m[0:1, grouped:grouped + 1].astype(F32)
    rinv = m[0:1, grouped + 64:grouped + 65].astype(F32)
    return decode(m[:, :feat], linv), decode(m[:, feat:grouped], rinv)


def kernel(
    tenant, storage, tok_in, w_in, cot_in, ain, aout,
    proj, tgrad_out, gin, gout,
    tok, w, cot, tgrad, gtotal,
    maps, sel, cnt, cotf, tokp, wp, base, rs_out, rs_right, rs_left,
    part, part_in, full, gx, gown, gz_out, gz_in,
    ssem, rsem, lsem,
):
    r, t = lax.axis_index("rep"), lax.axis_index("tp")
    z, x = lax.div(r, NX), lax.rem(r, NX)
    y, c = lax.div(t, NC), lax.rem(t, NC)
    rows = tok.shape[0]
    half = rows // 2
    nb = rows // BLOCK
    feat = tok.shape[1]
    rank = ain.shape[1]
    grouped = feat + cot.shape[1]
    other = 1 - c

    def at_y(d):
        return (r, lax.rem(y + d + NY, NY) * NC + c)

    def at_x(d):
        return (z * NX + lax.rem(x + d + NX, NX), t)

    def at_z(d):
        return (lax.rem(z + d + NZ, NZ) * NX + x, t)

    mate = (r, y * NC + other)
    counter = [0]
    sent = []

    def copy_to(src, dst, device):
        i = counter[0]
        counter[0] += 1
        made = pltpu.make_async_remote_copy(
            src_ref=src, dst_ref=dst, send_sem=ssem.at[i], recv_sem=rsem.at[i],
            device_id=device, device_id_type=MESH,
        )
        made.start()
        sent.append(made)
        return made

    own_lanes = pl.ds(pl.multiple_of(c * 128, 128), 128)
    local = [
        pltpu.make_async_copy(ain.at[0], maps.at[r, :, pl.ds(0, feat)], lsem.at[0]),
        pltpu.make_async_copy(aout.at[0], maps.at[r, :, pl.ds(feat, grouped - feat)], lsem.at[1]),
        pltpu.make_async_copy(cot_in, cot, lsem.at[2]),
        pltpu.make_async_copy(cot_in, cotf.at[y, :, own_lanes], lsem.at[3]),
        pltpu.make_async_copy(tok_in, tok, lsem.at[4]),
        pltpu.make_async_copy(w_in, w, lsem.at[5]),
    ]
    for made in local:
        made.start()

    barrier = pltpu.get_barrier_semaphore()
    greeted = [at_z(k) for k in (4, 3, 5, 2, 6, 1, 7)] + [at_x(2), at_x(1), at_x(3), at_y(1), at_y(-1), mate]
    for device in greeted:
        pl.semaphore_signal(barrier, inc=1, device_id=device, device_id_type=MESH)
    lane = lax.broadcasted_iota(jnp.int32, (1, 128), 1)
    slots = [storage[tenant[b]] for b in range(nb)]
    for b in range(nb):
        sel[0, b:b + 1, :] = jnp.where(lane == slots[b], 1.0, 0.0).astype(F32)
    for made in local:
        made.wait()
    pl.semaphore_wait(barrier, len(greeted))

    maps_z = {k: copy_to(maps.at[r], maps.at[r], at_z(k)) for k in (4, 3, 5, 2, 6, 1, 7)}
    maps_x = [copy_to(maps.at[r], maps.at[r], at_x(k)) for k in (2, 1, 3)]

    def cot_at(yy, cc, lo, size):
        return cotf.at[yy, pl.ds(lo, size), pl.ds(pl.multiple_of(cc * 128, 128), 128)]

    ag_right, ag_left, ag_mate = {}, {}, []
    ag_right[1] = copy_to(cot, cot_at(y, c, 0, rows), at_y(1))
    ag_left[1] = copy_to(cot, cot_at(y, c, 0, rows), at_y(-1))
    tok_mate = copy_to(tok, tokp, mate)
    pairs = ((4, 3), (5, 2), (6, 1), (7, 0))
    w_mate = {}

    def w_cols(d, cc):
        yy = lax.rem(y + d, NY)
        return pl.ds(pl.multiple_of(yy * (NC * 128) + cc * 128, 128), 128)

    for d in (4, 3, 5, 2, 6, 1, 7, 0):
        w_mate[d] = copy_to(w.at[:, w_cols(d, other)], wp.at[d], mate)
    ag_mate.append(copy_to(cot, cot_at(y, c, 0, rows), mate))
    sel_x = [copy_to(sel.at[0], sel.at[k], at_x(k)) for k in (1, 2, 3)]

    def own_pair(pair):
        both = dot(tok[...], jnp.concatenate([w[:, w_cols(d, c)] for d in pair], axis=1))
        base[pair[0]] = both[:, :128]
        base[pair[1]] = both[:, 128:]

    def mate_pair(pair):
        for d in pair:
            w_mate[d].wait_recv()
        both = dot(tokp[...], jnp.concatenate([wp[d] for d in pair], axis=1))
        base[pair[0]] += both[:, :128]
        base[pair[1]] += both[:, 128:]

    def maps_on(*ks):
        for k in ks:
            maps_z[k].wait_recv()
            came = maps.at[lax.rem(z - k + NZ, NZ) * NX + x]
            for j in (2, 1, 3):
                maps_x.append(copy_to(came, came, at_x(j)))

    def ag_step(s):
        ag_right[s].wait_recv()
        ag_left[s].wait_recv()
        lo_y, hi_y = lax.rem(y - s + NY, NY), lax.rem(y + s, NY)
        size = rows if s < 3 else half
        piece = cot_at(lo_y, c, 0, size)
        ag_right[s + 1] = copy_to(piece, piece, at_y(1))
        piece = cot_at(hi_y, c, rows - size, size)
        ag_left[s + 1] = copy_to(piece, piece, at_y(-1))
        for yy in (lo_y, hi_y):
            piece = cot_at(yy, c, 0, rows)
            ag_mate.append(copy_to(piece, piece, mate))

    rs = {}

    def rs_rows(h):
        return pl.ds(0 if h == "A" else half, half)

    def rs_send(way, h, d):
        slot = len([k for k in rs if k[0] == way])
        target = rs_right if way > 0 else rs_left
        place = slot + (7 if way < 0 else 0)
        code, inverse = encode(base[(way * d) % NY, rs_rows(h), :])
        rs_out[place, :half, :] = code
        rs_out[place, half:, :] = jnp.broadcast_to(inverse, (16, 128)).astype(BF16)
        made = copy_to(rs_out.at[place], target.at[slot], at_y(way))
        rs[way, h, d] = (made, slot)

    def rs_take(way, h, d):
        made, slot = rs[way, h, d]
        made.wait_recv()
        source = rs_right if way > 0 else rs_left
        inverse = source[slot, half:half + 1, :].astype(F32)
        base[(way * (d - 1)) % NY, rs_rows(h), :] += decode(source[slot, :half, :], inverse)

    def rs_hop(d, first):
        right, left = ("A", "B") if first else ("B", "A")
        rs_take(1, right, d + 1)
        rs_send(1, right, d)
        rs_take(-1, left, d + 1)
        rs_send(-1, left, d)

    def through(yy):
        tgrad[...] += dot_nt(cotf[yy], w[:, pl.ds(pl.multiple_of(yy * 256, 256), 256)])

    def through_steps(*pieces):
        for i, s in pieces:
            ag_mate[i].wait_recv()
            through(lax.rem(y - s + NY, NY))

    own_pair(pairs[0])
    own_pair(pairs[1])
    maps_on(1, 7, 2, 6)
    own_pair(pairs[2])
    maps_on(3, 5, 4)
    ag_step(1)
    tok_mate.wait_recv()
    mate_pair(pairs[0])
    rs_send(1, "A", 4)
    rs_send(-1, "B", 4)
    rs_send(1, "B", 3)
    mate_pair(pairs[1])
    rs_send(-1, "A", 3)
    own_pair(pairs[3])
    ag_step(2)

    for made in maps_x:
        made.wait_recv()
    chosen = [maps[slots[b]] for b in range(nb)]
    for b in range(0, nb, 2):
        here = pl.ds(b * BLOCK, 2 * BLOCK)
        two = jnp.concatenate([chosen[b], chosen[b + 1]], axis=0)
        pin = dot_nt(two[:, :feat], tok[here, :])
        pback = dot_nt(two[:, feat:], cot[here, :])
        for i in range(2):
            mine = slice(i * BLOCK, (i + 1) * BLOCK)
            part[b + i] = pin[rank * i:rank * i + 8, mine]
            part[nb + b + i] = pin[rank * i + 8:rank * i + 16, mine]
            part[2 * nb + b + i] = pback[rank * i:rank * i + 8, mine]
            part[3 * nb + b + i] = pback[rank * i + 8:rank * i + 16, mine]

    ag_step(3)
    ag_right[4].wait_recv()
    ag_left[4].wait_recv()
    far = cot_at(lax.rem(y + 4, NY), c, 0, rows)
    ag_mate.append(copy_to(far, far, mate))

    sums = []
    for k in (8, 7, 9, 6, 10, 5, 11, 4, 12, 3, 13, 2, 14, 1, 15):
        tt = lax.rem(t + k, NT)
        sums.append(copy_to(part.at[tt], part_in.at[k], (r, tt)))

    for made in sel_x:
        made.wait_recv()
    cnt[0] = jnp.sum(jnp.sum(sel[...], axis=0), axis=0, keepdims=True)
    counted = [copy_to(cnt.at[0], cnt.at[k], at_z(k)) for k in range(1, NZ)]

    mate_pair(pairs[2])
    rs_hop(3, True)
    rs_hop(2, False)

    total = part[t]
    for made in sums:
        made.wait_recv()
    for k in range(1, NT):
        total = total + part_in[k]
    full[t] = total
    spread = []
    for k in (8, 7, 9, 6, 10, 5, 11, 4, 12, 3, 13, 2, 14, 1, 15):
        spread.append(copy_to(full.at[t], full.at[t], (r, lax.rem(t + k, NT))))

    mate_pair(pairs[3])
    rs_hop(2, True)
    ag_mate[0].wait_recv()
    tgrad[...] = dot_nt(cotf[y], w[:, pl.ds(pl.multiple_of(y * 256, 256), 256)])
    through_steps((1, 1), (2, -1))

    for made in spread:
        made.wait_recv()
    rin = [two_parts(jnp.concatenate([full[b], full[nb + b]], axis=0)) for b in range(nb)]
    rback = [two_parts(jnp.concatenate([full[2 * nb + b], full[3 * nb + b]], axis=0)) for b in range(nb)]
    for b in range(nb):
        here = pl.ds(b * BLOCK, BLOCK)
        da = dot(rback[b], tok[here, :])
        db = dot(rin[b], cot[here, :])
        own = jnp.concatenate([da[:rank] + da[rank:], db[:rank] + db[rank:]], axis=1)
        gown[b] = own
        gx[0, b] = encode_grads(own, feat)
    grads_x = [copy_to(gx.at[0], gx.at[k], at_x(k)) for k in (2, 1, 3)]

    rs_hop(1, False)
    for b in range(nb):
        here = pl.ds(b * BLOCK, BLOCK)
        amap = jnp.concatenate([chosen[b][:, :feat]] * 2, axis=0)
        bmap = jnp.concatenate([chosen[b][:, feat:]] * 2, axis=0)
        tgrad[here, :] += 2.0 * dot_tn(rback[b], amap)
        base[0, here, :] += 2.0 * dot_tn(rin[b], bmap)
    rs_hop(1, True)
    through_steps((3, 2), (4, -2))

    for made in grads_x:
        made.wait_recv()
    for k in range(1, NX):
        for b in range(nb):
            one, two = decode_grads(gx[k, b], feat)
            gown[k * nb + b, :, :feat] = one
            gown[k * nb + b, :, feat:] = two
    grads_z = {}
    for d in (4, 3, 5, 2, 6, 1, 7, 0):
        owner = lax.rem(z + d, NZ) * NX + x
        acc = jnp.zeros((rank, grouped), F32)
        for k in range(NX):
            weight = jnp.sum(jnp.where(lane == owner, sel[k], 0.0), axis=1, keepdims=True)
            for b in range(nb):
                acc = acc + weight[b:b + 1, :] * gown[k * nb + b]
        if d:
            gz_out[d] = encode_grads(acc, feat)
            grads_z[d] = copy_to(gz_out.at[d], gz_in.at[d], at_z(d))
        else:
            gtotal[...] = acc

    through_steps((5, 3), (6, -3), (7, 4))
    out_tg = pltpu.make_async_copy(tgrad, tgrad_out, lsem.at[0])
    out_tg.start()

    rs_take(1, "B", 1)
    rs_take(-1, "A", 1)
    rs_take(1, "A", 1)
    rs_take(-1, "B", 1)
    out_pj = pltpu.make_async_copy(base.at[0], proj, lsem.at[1])
    out_pj.start()

    for made in counted:
        made.wait_recv()
    blocks_of = jnp.sum(cnt[...], axis=0)
    mine = jnp.sum(jnp.where(lane == r, blocks_of, 0.0), axis=1, keepdims=True)
    scale = 2.0 / jnp.maximum(mine * float(BLOCK), 1.0)
    acc_in, acc_out = gtotal[:, :feat], gtotal[:, feat:]
    for d in (1, 7, 2, 6, 3, 5, 4):
        grads_z[d].wait_recv()
        one, two = decode_grads(gz_in[d], feat)
        acc_in, acc_out = acc_in + one, acc_out + two
    gtotal[:, :feat] = acc_in * scale
    gtotal[:, feat:] = acc_out * scale
    out_gi = pltpu.make_async_copy(gtotal.at[:, pl.ds(0, feat)], gin.at[0], lsem.at[2])
    out_go = pltpu.make_async_copy(gtotal.at[:, pl.ds(feat, grouped - feat)], gout.at[0], lsem.at[3])
    out_gi.start()
    out_go.start()
    for made in (out_tg, out_pj, out_gi, out_go):
        made.wait()
    for made in sent:
        made.wait_send()


def finish(*refs):
    n = 4
    writes = [pltpu.make_async_copy(refs[i], refs[n + i], refs[2 * n].at[i]) for i in range(n)]
    for made in writes:
        made.start()
    for made in writes:
        made.wait()


COPIES = 128


def shards(tok, w, cot, ain, aout, tenant, storage):
    rows, feat = tok.shape
    cols = cot.shape[1]
    rank = ain.shape[1]
    nb = tenant.shape[0]
    grouped = feat + cols
    smem = pl.BlockSpec(memory_space=pltpu.SMEM)
    anywhere = pl.BlockSpec(memory_space=pl.ANY)
    shapes = ((rows, cols), (rows, feat), ain.shape, aout.shape)
    results = pl.pallas_call(
        kernel,
        out_shape=tuple(jax.ShapeDtypeStruct(shape, F32) for shape in shapes),
        in_specs=[smem, smem] + [anywhere] * 5,
        out_specs=[anywhere] * 4,
        scratch_shapes=[
            pltpu.VMEM((rows, feat), BF16),
            pltpu.VMEM(w.shape, BF16),
            pltpu.VMEM((rows, cols), BF16),
            pltpu.VMEM((rows, feat), F32),
            pltpu.VMEM((rank, grouped), F32),
            pltpu.VMEM((NX * NZ, rank, grouped), BF16),
            pltpu.VMEM((NX, nb, 128), F32),
            pltpu.VMEM((NZ, 1, 128), F32),
            pltpu.VMEM((NY, rows, NC * cols), BF16),
            pltpu.VMEM((rows, feat), BF16),
            pltpu.VMEM((NY, feat, cols), BF16),
            pltpu.VMEM((NY, rows, cols), F32),
            pltpu.VMEM((14, rows // 2 + 16, cols), BF16),
            pltpu.VMEM((7, rows // 2 + 16, cols), BF16),
            pltpu.VMEM((7, rows // 2 + 16, cols), BF16),
            pltpu.VMEM((NT, 8, 128), F32),
            pltpu.VMEM((NT, 8, 128), F32),
            pltpu.VMEM((NT, 8, 128), F32),
            pltpu.VMEM((NX, nb, rank, grouped + 128), BF16),
            pltpu.VMEM((NX * nb, rank, grouped), F32),
            pltpu.VMEM((NZ, rank, grouped + 128), BF16),
            pltpu.VMEM((NZ, rank, grouped + 128), BF16),
            pltpu.SemaphoreType.DMA((COPIES,)),
            pltpu.SemaphoreType.DMA((COPIES,)),
            pltpu.SemaphoreType.DMA((6,)),
        ],
        compiler_params=pltpu.CompilerParams(
            collective_id=0, has_side_effects=True, vmem_limit_bytes=VMEM_GRANT
        ),
    )(tenant, storage, tok, w, cot, ain, aout)
    return pl.pallas_call(
        finish,
        out_shape=tuple(jax.ShapeDtypeStruct(shape, F32) for shape in shapes),
        in_specs=[anywhere] * 4,
        out_specs=[anywhere] * 4,
        scratch_shapes=[pltpu.SemaphoreType.DMA((4,))],
        compiler_params=pltpu.CompilerParams(vmem_limit_bytes=2 * 1024 * 1024),
    )(*results)


VMEM_GRANT = 24 * 1024 * 1024


def solution(mesh):
    placed = (
        P("rep", "tp"),
        P("tp", None),
        P("rep", "tp"),
        P("rep", None, "tp"),
        P("rep", None, "tp"),
        P("rep"),
        P(),
    )
    return jax.shard_map(
        shards,
        mesh=mesh,
        in_specs=placed,
        out_specs=(P("rep", "tp"), P("rep", "tp"), P("rep", None, "tp"), P("rep", None, "tp")),
        check_vma=False,
    )
```

time: 78.4 us -> 71 us (0.906)
  Pallas kernels: 72.4 us -> 63.8 us
  local copies, waits for them, and re-layouts: 5.16 us -> 6.24 us
    pallas_call x1 -> x2, Pallas kernels: 72.4 us -> 63.8 us  [the longest x1 62.7 us: shards(): pl.pallas_call(kernel, out_shape=tuple((jax.ShapeDtypeStruct(shape, F32)...]
    unnamed x8 -> x14, local copies, waits for them, and re-layouts: 5.16 us -> 6.24 us
where the time goes in v2:
time: 71 us; the launch traced here: 70.7 us
  Pallas kernels  63.8 us (90%)
  local copies, waits for them, and re-layouts  6.24 us (9%)
    pallas_call x1, Pallas kernels, shards(): pl.pallas_call(kernel, out_shape=tuple((jax.ShapeDtypeStruct(shape, F32)...  62.7 us
    unnamed x14, local copies, waits for them, and re-layouts  6.24 us

profile of v2, /device:TPU:1, one launch (start us, length us, event | category | flops | bytes accessed | tf_op | source)
XLA Modules:
  0.0 70.7 jit_solution(12835201694788195023)
XLA Ops:
  0.6 0.0 copy-start
  0.6 1.6 %copy-done = bf16[512,2048]{1,0:T(8,128)(2,1)S(1)} copy-done((bf16[512,2048]{1,0:T(8,128)(2,1)S(1)}, bf16[512,2048]{1,0:T(8,128)(2,1)}, u32[]{:S(2)}) %copy-start) | copy-done | bytes 2097176
  2.2 0.0 copy-start.1
  2.2 1.0 %copy-done.1 = bf16[512,512]{1,0:T(8,128)(2,1)S(1)} copy-done((bf16[512,512]{1,0:T(8,128)(2,1)S(1)}, bf16[512,512]{1,0:T(8,128)(2,1)}, u32[]{:S(2)}) %copy-start.1) | copy-done | bytes 524312
  3.3 0.0 copy-start.2
  3.3 0.9 %copy-done.2 = bf16[512,128]{1,0:T(8,128)(2,1)S(1)} copy-done((bf16[512,128]{1,0:T(8,128)(2,1)S(1)}, bf16[512,128]{1,0:T(8,128)(2,1)}, u32[]{:S(2)}) %copy-start.2) | copy-done | bytes 131096
  4.2 0.0 copy-start.3
  4.2 0.7 %copy-done.3 = bf16[1,16,512]{2,1,0:T(8,128)(2,1)S(1)} copy-done((bf16[1,16,512]{2,1,0:T(8,128)(2,1)S(1)}, bf16[1,16,512]{2,1,0:T(8,128)(2,1)}, u32[]{:S(2)}) %copy-start.3) | copy-done | bytes 16408
  4.9 0.0 copy-start.4
  4.9 0.7 copy-done.4
  5.6 0.0 copy-start.5
  5.6 0.7 copy-done.5
  6.2 0.0 copy-start.6
  6.2 0.7 copy-done.6
  6.9 62.7 %shard_map.102 = (f32[512,128]{1,0:T(8,128)S(1)}, f32[512,512]{1,0:T(8,128)S(1)}, f32[1,16,512]{2,1,0:T(8,128)S(1)}, f32[1,16,128]{2,1,0:T(8,128)S(1)}) custom-call(s32[4]{0:T(128)S(1)} %copy-done.5, s32[32]{0:T(128)S(1)} %copy-done.6, bf16[512,512]{1,0:T(8,128)(2,1)S(1)} %copy-done.1, bf16[512,2048]{1,0:T(8,128)(2,1)S(1)} %copy-done, ...), custom_call_target="tpu_custom_call" | custom-call | tf_op jit(solution)/shard_map/pallas_call | solution.py:396
  69.6 1.1 %shard_map.103 = (f32[512,128]{1,0:T(8,128)}, f32[512,512]{1,0:T(8,128)}, f32[1,16,512]{2,1,0:T(8,128)}, f32[1,16,128]{2,1,0:T(8,128)}) custom-call(f32[512,128]{1,0:T(8,128)S(1)} %get-tuple-element.8.refs_0_, f32[512,512]{1,0:T(8,128)S(1)} %get-tuple-element.9.refs_1_, f32[1,16,512]{2,1,0:T(8,128)S(1)} %get-tuple-element.10.refs_2_, ...), custom_call_target="tpu_custom_call" | custom-call | tf_op jit(solution)/shard_map/pallas_call | solution.py:432
Async XLA Ops:
  0.6 1.6 %copy-start = (bf16[512,2048]{1,0:T(8,128)(2,1)S(1)}, bf16[512,2048]{1,0:T(8,128)(2,1)}, u32[]{:S(2)}) copy-start(bf16[512,2048]{1,0:T(8,128)(2,1)} %w_in.1) | copy-start | bytes 6291460
  2.2 1.0 %copy-start.1 = (bf16[512,512]{1,0:T(8,128)(2,1)S(1)}, bf16[512,512]{1,0:T(8,128)(2,1)}, u32[]{:S(2)}) copy-start(bf16[512,512]{1,0:T(8,128)(2,1)} %tok_in.1) | copy-start | bytes 1572868
  3.3 0.9 %copy-start.2 = (bf16[512,128]{1,0:T(8,128)(2,1)S(1)}, bf16[512,128]{1,0:T(8,128)(2,1)}, u32[]{:S(2)}) copy-start(bf16[512,128]{1,0:T(8,128)(2,1)} %cot_in.1) | copy-start | bytes 393220
  4.2 0.7 %copy-start.3 = (bf16[1,16,512]{2,1,0:T(8,128)(2,1)S(1)}, bf16[1,16,512]{2,1,0:T(8,128)(2,1)}, u32[]{:S(2)}) copy-start(bf16[1,16,512]{2,1,0:T(8,128)(2,1)} %ain.1) | copy-start | bytes 49156
  4.9 0.7 copy-start.4
  5.6 0.7 copy-start.5
  6.2 0.7 copy-start.6

commit v3 on v2

--- a/solution.py
+++ b/solution.py
@@ -126,18 +126,29 @@
         made.start()
 
     barrier = pltpu.get_barrier_semaphore()
-    greeted = [at_z(k) for k in (4, 3, 5, 2, 6, 1, 7)] + [at_x(2), at_x(1), at_x(3), at_y(1), at_y(-1), mate]
+    greeted = [at_z(k) for k in (4, 3, 5, 2, 6, 1, 7)] + [at_x(2), at_x(1), at_x(3)]
+    greeted += [(r, lax.rem(t + k, NT)) for k in range(1, NT)]
     for device in greeted:
         pl.semaphore_signal(barrier, inc=1, device_id=device, device_id_type=MESH)
     lane = lax.broadcasted_iota(jnp.int32, (1, 128), 1)
     slots = [storage[tenant[b]] for b in range(nb)]
     for b in range(nb):
         sel[0, b:b + 1, :] = jnp.where(lane == slots[b], 1.0, 0.0).astype(F32)
+    pairs = ((4, 3), (5, 2), (6, 1), (7, 0))
+
+    def w_cols(d, cc):
+        yy = lax.rem(y + d, NY)
+        return pl.ds(pl.multiple_of(yy * (NC * 128) + cc * 128, 128), 128)
+
     for made in local:
         made.wait()
+    for pair in pairs:
+        both = dot(tok[...], jnp.concatenate([w[:, w_cols(d, c)] for d in pair], axis=1))
+        base[pair[0]] = both[:, :128]
+        base[pair[1]] = both[:, 128:]
     pl.semaphore_wait(barrier, len(greeted))
 
-    maps_z = {k: copy_to(maps.at[r], maps.at[r], at_z(k)) for k in (4, 3, 5, 2, 6, 1, 7)}
+    maps_z = {k: copy_to(maps.at[r], maps.at[r], at_z(k)) for k in (1, 7, 2, 6, 3, 5, 4)}
     maps_x = [copy_to(maps.at[r], maps.at[r], at_x(k)) for k in (2, 1, 3)]
 
     def cot_at(yy, cc, lo, size):
@@ -147,22 +158,12 @@
     ag_right[1] = copy_to(cot, cot_at(y, c, 0, rows), at_y(1))
     ag_left[1] = copy_to(cot, cot_at(y, c, 0, rows), at_y(-1))
     tok_mate = copy_to(tok, tokp, mate)
-    pairs = ((4, 3), (5, 2), (6, 1), (7, 0))
     w_mate = {}
-
-    def w_cols(d, cc):
-        yy = lax.rem(y + d, NY)
-        return pl.ds(pl.multiple_of(yy * (NC * 128) + cc * 128, 128), 128)
 
     for d in (4, 3, 5, 2, 6, 1, 7, 0):
         w_mate[d] = copy_to(w.at[:, w_cols(d, other)], wp.at[d], mate)
     ag_mate.append(copy_to(cot, cot_at(y, c, 0, rows), mate))
     sel_x = [copy_to(sel.at[0], sel.at[k], at_x(k)) for k in (1, 2, 3)]
-
-    def own_pair(pair):
-        both = dot(tok[...], jnp.concatenate([w[:, w_cols(d, c)] for d in pair], axis=1))
-        base[pair[0]] = both[:, :128]
-        base[pair[1]] = both[:, 128:]
 
     def mate_pair(pair):
         for d in pair:
@@ -228,21 +229,28 @@
             ag_mate[i].wait_recv()
             through(lax.rem(y - s + NY, NY))
 
-    own_pair(pairs[0])
-    own_pair(pairs[1])
-    maps_on(1, 7, 2, 6)
-    own_pair(pairs[2])
-    maps_on(3, 5, 4)
-    ag_step(1)
     tok_mate.wait_recv()
     mate_pair(pairs[0])
     rs_send(1, "A", 4)
     rs_send(-1, "B", 4)
     rs_send(1, "B", 3)
+    maps_on(1, 7)
     mate_pair(pairs[1])
     rs_send(-1, "A", 3)
-    own_pair(pairs[3])
+    maps_on(2, 6)
+    ag_step(1)
+    mate_pair(pairs[2])
+    maps_on(3, 5)
+    mate_pair(pairs[3])
+    maps_on(4)
+    rs_hop(3, True)
     ag_step(2)
+    rs_hop(2, False)
+    for made in sel_x:
+        made.wait_recv()
+    cnt[0] = jnp.sum(jnp.sum(sel[...], axis=0), axis=0, keepdims=True)
+    counted = [copy_to(cnt.at[0], cnt.at[k], at_z(k)) for k in range(1, NZ)]
+    rs_hop(2, True)
 
     for made in maps_x:
         made.wait_recv()
@@ -259,25 +267,16 @@
             part[2 * nb + b + i] = pback[rank * i:rank * i + 8, mine]
             part[3 * nb + b + i] = pback[rank * i + 8:rank * i + 16, mine]
 
-    ag_step(3)
-    ag_right[4].wait_recv()
-    ag_left[4].wait_recv()
-    far = cot_at(lax.rem(y + 4, NY), c, 0, rows)
-    ag_mate.append(copy_to(far, far, mate))
-
     sums = []
     for k in (8, 7, 9, 6, 10, 5, 11, 4, 12, 3, 13, 2, 14, 1, 15):
         tt = lax.rem(t + k, NT)
         sums.append(copy_to(part.at[tt], part_in.at[k], (r, tt)))
 
-    for made in sel_x:
-        made.wait_recv()
-    cnt[0] = jnp.sum(jnp.sum(sel[...], axis=0), axis=0, keepdims=True)
-    counted = [copy_to(cnt.at[0], cnt.at[k], at_z(k)) for k in range(1, NZ)]
-
-    mate_pair(pairs[2])
-    rs_hop(3, True)
-    rs_hop(2, False)
+    ag_step(3)
+    rs_hop(1, False)
+    ag_mate[0].wait_recv()
+    tgrad[...] = dot_nt(cotf[y], w[:, pl.ds(pl.multiple_of(y * 256, 256), 256)])
+    through_steps((1, 1))
 
     total = part[t]
     for made in sums:
@@ -289,11 +288,12 @@
     for k in (8, 7, 9, 6, 10, 5, 11, 4, 12, 3, 13, 2, 14, 1, 15):
         spread.append(copy_to(full.at[t], full.at[t], (r, lax.rem(t + k, NT))))
 
-    mate_pair(pairs[3])
-    rs_hop(2, True)
-    ag_mate[0].wait_recv()
-    tgrad[...] = dot_nt(cotf[y], w[:, pl.ds(pl.multiple_of(y * 256, 256), 256)])
-    through_steps((1, 1), (2, -1))
+    rs_hop(1, True)
+    ag_right[4].wait_recv()
+    ag_left[4].wait_recv()
+    far = cot_at(lax.rem(y + 4, NY), c, 0, rows)
+    ag_mate.append(copy_to(far, far, mate))
+    through_steps((2, -1), (3, 2), (4, -2))
 
     for made in spread:
         made.wait_recv()
@@ -308,15 +308,13 @@
         gx[0, b] = encode_grads(own, feat)
     grads_x = [copy_to(gx.at[0], gx.at[k], at_x(k)) for k in (2, 1, 3)]
 
-    rs_hop(1, False)
     for b in range(nb):
         here = pl.ds(b * BLOCK, BLOCK)
         amap = jnp.concatenate([chosen[b][:, :feat]] * 2, axis=0)
         bmap = jnp.concatenate([chosen[b][:, feat:]] * 2, axis=0)
         tgrad[here, :] += 2.0 * dot_tn(rback[b], amap)
         base[0, here, :] += 2.0 * dot_tn(rin[b], bmap)
-    rs_hop(1, True)
-    through_steps((3, 2), (4, -2))
+    through_steps((5, 3), (6, -3))
 
     for made in grads_x:
         made.wait_recv()
@@ -339,7 +337,7 @@
         else:
             gtotal[...] = acc
 
-    through_steps((5, 3), (6, -3), (7, 4))
+    through_steps((7, 4))
     out_tg = pltpu.make_async_copy(tgrad, tgrad_out, lsem.at[0])
     out_tg.start()
 
@@ -374,9 +372,14 @@
 
 def finish(*refs):
     n = 4
-    writes = [pltpu.make_async_copy(refs[i], refs[n + i], refs[2 * n].at[i]) for i in range(n)]
-    for made in writes:
+    sources, targets, held, came, gone = refs[:n], refs[n:2 * n], refs[2 * n:3 * n], refs[3 * n], refs[3 * n + 1]
+    reads = [pltpu.make_async_copy(sources[i], held[i], came.at[i]) for i in range(n)]
+    writes = [pltpu.make_async_copy(held[i], targets[i], gone.at[i]) for i in range(n)]
+    for made in reads:
         made.start()
+    for i in range(n):
+        reads[i].wait()
+        writes[i].start()
     for made in writes:
         made.wait()
 
@@ -434,12 +437,13 @@
         out_shape=tuple(jax.ShapeDtypeStruct(shape, F32) for shape in shapes),
         in_specs=[anywhere] * 4,
         out_specs=[anywhere] * 4,
-        scratch_shapes=[pltpu.SemaphoreType.DMA((4,))],
-        compiler_params=pltpu.CompilerParams(vmem_limit_bytes=2 * 1024 * 1024),
+        scratch_shapes=[pltpu.VMEM(shape, F32) for shape in shapes]
+        + [pltpu.SemaphoreType.DMA((4,)), pltpu.SemaphoreType.DMA((4,))],
+        compiler_params=pltpu.CompilerParams(vmem_limit_bytes=VMEM_GRANT),
     )(*results)
 
 
-VMEM_GRANT = 24 * 1024 * 1024
+VMEM_GRANT = 63 * 1024 * 1024
 
 
 def solution(mesh):

time: 71 us -> 64.1 us (0.903)
  local copies, waits for them, and re-layouts: 6.24 us -> 0 us
    unnamed x14 -> x0, local copies, waits for them, and re-layouts: 6.24 us -> none
    pallas_call x1, Pallas kernels: 62.7 us -> 60.9 us  [shards(): pl.pallas_call(kernel, out_shape=tuple((jax.ShapeDtypeStruct(shape, F32)...]
    pallas_call x1, Pallas kernels: 1.1 us -> 2.36 us  [shards(): pl.pallas_call(finish, out_shape=tuple((jax.ShapeDtypeStruct(shape, F32)...]
where the time goes in v3:
time: 64.1 us; the launch traced here: 63.9 us
  Pallas kernels  63.2 us (99%)
    pallas_call x1, Pallas kernels, shards(): pl.pallas_call(kernel, out_shape=tuple((jax.ShapeDtypeStruct(shape, F32)...  60.9 us
    pallas_call x1, Pallas kernels, shards(): pl.pallas_call(finish, out_shape=tuple((jax.ShapeDtypeStruct(shape, F32)...  2.36 us

profile of v3, /device:TPU:1, one launch (start us, length us, event | category | flops | bytes accessed | tf_op | source)
XLA Modules:
  0.0 63.9 jit_solution(83044558411053953)
XLA Ops:
  0.6 60.9 %shard_map.102 = (f32[512,128]{1,0:T(8,128)}, f32[512,512]{1,0:T(8,128)}, f32[1,16,512]{2,1,0:T(8,128)}, f32[1,16,128]{2,1,0:T(8,128)}) custom-call(s32[4]{0:T(128)} %tenant.1, s32[32]{0:T(128)} %storage.1, bf16[512,512]{1,0:T(8,128)(2,1)} %tok_in.1, bf16[512,2048]{1,0:T(8,128)(2,1)} %w_in.1, bf16[512,128]{1,0:T(8,128)(2,1)} %cot_in.1, ...), custom_call_target="tpu_custom_call" | custom-call | tf_op jit(solution)/shard_map/pallas_call | solution.py:399
  61.5 2.4 %shard_map.103 = (f32[512,128]{1,0:T(8,128)}, f32[512,512]{1,0:T(8,128)}, f32[1,16,512]{2,1,0:T(8,128)}, f32[1,16,128]{2,1,0:T(8,128)}) custom-call(f32[512,128]{1,0:T(8,128)} %get-tuple-element.8.refs_0_, f32[512,512]{1,0:T(8,128)} %get-tuple-element.9.refs_1_, f32[1,16,512]{2,1,0:T(8,128)} %get-tuple-element.10.refs_2_, ...), custom_call_target="tpu_custom_call" | custom-call | tf_op jit(solution)/shard_map/pallas_call | solution.py:435

commit v4 on v3

--- a/solution.py
+++ b/solution.py
@@ -53,29 +53,23 @@
     return jnp.where(y < 0, -p, p) * inverse
 
 
-def encode_grads(v, feat):
-    left, linv = encode(v[:, :feat])
-    right, rinv = encode(v[:, feat:])
-    rank = v.shape[0]
-    tail = jnp.concatenate(
-        [jnp.broadcast_to(linv, (rank, 64)), jnp.broadcast_to(rinv, (rank, 64))], axis=1
-    )
-    return jnp.concatenate([left, right, tail.astype(BF16)], axis=1)
-
-
-def decode_grads(m, feat):
-    grouped = m.shape[1] - 128
-    linv = m[0:1, grouped:grouped + 1].astype(F32)
-    rinv = m[0:1, grouped + 64:grouped + 65].astype(F32)
-    return decode(m[:, :feat], linv), decode(m[:, feat:grouped], rinv)
+def encode_wide(v):
+    code, inverse = encode(v)
+    tail = jnp.broadcast_to(inverse, (v.shape[0], 128)).astype(BF16)
+    return jnp.concatenate([code, tail], axis=1)
+
+
+def decode_wide(m):
+    n = m.shape[1] - 128
+    return decode(m[:, :n], m[0:1, n:n + 1].astype(F32))
 
 
 def kernel(
     tenant, storage, tok_in, w_in, cot_in, ain, aout,
     proj, tgrad_out, gin, gout,
     tok, w, cot, tgrad, gtotal,
-    maps, sel, cnt, cotf, tokp, wp, base, rs_out, rs_right, rs_left,
-    part, part_in, full, gx, gown, gz_out, gz_in,
+    maps_a, maps_b, sel, cnt, cotf, tokp, wp, base, rs_out, rs_right, rs_left,
+    part, part_in, full, gxa, gxb, owna, ownb, za_out, zb_out, za_in, zb_in,
     ssem, rsem, lsem,
 ):
     r, t = lax.axis_index("rep"), lax.axis_index("tp")
@@ -115,8 +109,8 @@
 
     own_lanes = pl.ds(pl.multiple_of(c * 128, 128), 128)
     local = [
-        pltpu.make_async_copy(ain.at[0], maps.at[r, :, pl.ds(0, feat)], lsem.at[0]),
-        pltpu.make_async_copy(aout.at[0], maps.at[r, :, pl.ds(feat, grouped - feat)], lsem.at[1]),
+        pltpu.make_async_copy(ain.at[0], maps_a.at[r], lsem.at[0]),
+        pltpu.make_async_copy(aout.at[0], maps_b.at[r], lsem.at[1]),
         pltpu.make_async_copy(cot_in, cot, lsem.at[2]),
         pltpu.make_async_copy(cot_in, cotf.at[y, :, own_lanes], lsem.at[3]),
         pltpu.make_async_copy(tok_in, tok, lsem.at[4]),
@@ -140,16 +134,16 @@
         yy = lax.rem(y + d, NY)
         return pl.ds(pl.multiple_of(yy * (NC * 128) + cc * 128, 128), 128)
 
-    for made in local:
+    for made in local[:4]:
         made.wait()
-    for pair in pairs:
-        both = dot(tok[...], jnp.concatenate([w[:, w_cols(d, c)] for d in pair], axis=1))
-        base[pair[0]] = both[:, :128]
-        base[pair[1]] = both[:, 128:]
     pl.semaphore_wait(barrier, len(greeted))
 
-    maps_z = {k: copy_to(maps.at[r], maps.at[r], at_z(k)) for k in (1, 7, 2, 6, 3, 5, 4)}
-    maps_x = [copy_to(maps.at[r], maps.at[r], at_x(k)) for k in (2, 1, 3)]
+    near_z, near_x = (1, 7, 2, 6, 3, 5, 4), (2, 1, 3)
+    along_z, along_x = {}, {}
+    for kind, maps in (("b", maps_b), ("a", maps_a)):
+        for k in near_z:
+            along_z[kind, k] = copy_to(maps.at[r], maps.at[r], at_z(k))
+        along_x[kind] = [copy_to(maps.at[r], maps.at[r], at_x(k)) for k in near_x]
 
     def cot_at(yy, cc, lo, size):
         return cotf.at[yy, pl.ds(lo, size), pl.ds(pl.multiple_of(cc * 128, 128), 128)]
@@ -157,6 +151,8 @@
     ag_right, ag_left, ag_mate = {}, {}, []
     ag_right[1] = copy_to(cot, cot_at(y, c, 0, rows), at_y(1))
     ag_left[1] = copy_to(cot, cot_at(y, c, 0, rows), at_y(-1))
+    for made in local[4:]:
+        made.wait()
     tok_mate = copy_to(tok, tokp, mate)
     w_mate = {}
 
@@ -172,12 +168,95 @@
         base[pair[0]] += both[:, :128]
         base[pair[1]] += both[:, 128:]
 
-    def maps_on(*ks):
+    def own_pair(pair):
+        both = dot(tok[...], jnp.concatenate([w[:, w_cols(d, c)] for d in pair], axis=1))
+        base[pair[0]] = both[:, :128]
+        base[pair[1]] = both[:, 128:]
+
+    def maps_on(kind, *ks):
+        maps = maps_a if kind == "a" else maps_b
         for k in ks:
-            maps_z[k].wait_recv()
+            along_z[kind, k].wait_recv()
             came = maps.at[lax.rem(z - k + NZ, NZ) * NX + x]
-            for j in (2, 1, 3):
-                maps_x.append(copy_to(came, came, at_x(j)))
+            for j in near_x:
+                along_x[kind].append(copy_to(came, came, at_x(j)))
+
+    def blocks_of(i):
+        return pl.ds(i * BLOCK, BLOCK)
+
+    far_first = (8, 7, 9, 6, 10, 5, 11, 4, 12, 3, 13, 2, 14, 1, 15)
+    sums, spread = {}, {}
+
+    def rank_start(i, kind, maps, data):
+        for made in along_x[kind]:
+            made.wait_recv()
+        chosen = [maps[slots[b]] for b in range(nb)]
+        for b in range(0, nb, 2):
+            two = jnp.concatenate([chosen[b], chosen[b + 1]], axis=0)
+            both = dot_nt(two, data[pl.ds(b * BLOCK, 2 * BLOCK), :])
+            for h in range(2):
+                for j in range(4):
+                    lo = rank * h + 4 * j
+                    part[i, j * nb + b + h] = both[lo:lo + 4, h * BLOCK:(h + 1) * BLOCK]
+        sums[i] = []
+        for k in far_first:
+            tt = lax.rem(t + k, NT)
+            sums[i].append(copy_to(part.at[i, tt], part_in.at[i, k], (r, tt)))
+        return chosen
+
+    def rank_middle(i):
+        total = part[i, t]
+        for made in sums[i]:
+            made.wait_recv()
+        for k in range(1, NT):
+            total = total + part_in[i, k]
+        full[i, t] = total
+        spread[i] = [copy_to(full.at[i, t], full.at[i, t], (r, lax.rem(t + k, NT))) for k in far_first]
+
+    def rank_end(i):
+        for made in spread[i]:
+            made.wait_recv()
+        return [
+            two_parts(jnp.concatenate([full[i, j * nb + b] for j in range(4)], axis=0))
+            for b in range(nb)
+        ]
+
+    def grads_start(ranks, data, gx, own):
+        for b in range(nb):
+            g = dot(ranks[b], data[blocks_of(b), :])
+            g = g[:rank] + g[rank:]
+            own[b] = g
+            gx[0, b] = encode_wide(g)
+        return [copy_to(gx.at[0], gx.at[k], at_x(k)) for k in near_x]
+
+    def grads_middle(going, gx, own, out, into, lo):
+        for made in going:
+            made.wait_recv()
+        for k in range(1, NX):
+            for b in range(nb):
+                own[k * nb + b] = decode_wide(gx[k, b])
+        made = {}
+        n = own.shape[2]
+        for d in near_z + (0,):
+            owner = lax.rem(z + d, NZ) * NX + x
+            acc = jnp.zeros((rank, n), F32)
+            for k in range(NX):
+                weight = jnp.sum(jnp.where(lane == owner, sel[k], 0.0), axis=1, keepdims=True)
+                for b in range(nb):
+                    acc = acc + weight[b:b + 1, :] * own[k * nb + b]
+            if d:
+                out[d] = encode_wide(acc)
+                made[d] = copy_to(out.at[d], into.at[d], at_z(d))
+            else:
+                gtotal[:, lo:lo + n] = acc
+        return made
+
+    def grads_end(going, into, lo, n, scale):
+        acc = gtotal[:, lo:lo + n]
+        for d in near_z:
+            going[d].wait_recv()
+            acc = acc + decode_wide(into[d])
+        gtotal[:, lo:lo + n] = acc * scale
 
     def ag_step(s):
         ag_right[s].wait_recv()
@@ -229,137 +308,78 @@
             ag_mate[i].wait_recv()
             through(lax.rem(y - s + NY, NY))
 
+    maps_on("b", 1, 7)
+    own_pair(pairs[0])
+    maps_on("b", 2, 6)
+    maps_on("a", 1, 7)
+    own_pair(pairs[1])
     tok_mate.wait_recv()
     mate_pair(pairs[0])
     rs_send(1, "A", 4)
     rs_send(-1, "B", 4)
+    maps_on("b", 3, 5)
+    maps_on("a", 2, 6)
+    maps_on("b", 4)
     rs_send(1, "B", 3)
-    maps_on(1, 7)
     mate_pair(pairs[1])
     rs_send(-1, "A", 3)
-    maps_on(2, 6)
     ag_step(1)
+    maps_on("a", 3, 5)
+    maps_on("a", 4)
+    chosen_b = rank_start(0, "b", maps_b, cot)
+    own_pair(pairs[2])
+    own_pair(pairs[3])
     mate_pair(pairs[2])
-    maps_on(3, 5)
-    mate_pair(pairs[3])
-    maps_on(4)
     rs_hop(3, True)
     ag_step(2)
+    chosen_a = rank_start(1, "a", maps_a, tok)
+    rank_middle(0)
+    mate_pair(pairs[3])
     rs_hop(2, False)
     for made in sel_x:
         made.wait_recv()
     cnt[0] = jnp.sum(jnp.sum(sel[...], axis=0), axis=0, keepdims=True)
     counted = [copy_to(cnt.at[0], cnt.at[k], at_z(k)) for k in range(1, NZ)]
     rs_hop(2, True)
-
-    for made in maps_x:
-        made.wait_recv()
-    chosen = [maps[slots[b]] for b in range(nb)]
-    for b in range(0, nb, 2):
-        here = pl.ds(b * BLOCK, 2 * BLOCK)
-        two = jnp.concatenate([chosen[b], chosen[b + 1]], axis=0)
-        pin = dot_nt(two[:, :feat], tok[here, :])
-        pback = dot_nt(two[:, feat:], cot[here, :])
-        for i in range(2):
-            mine = slice(i * BLOCK, (i + 1) * BLOCK)
-            part[b + i] = pin[rank * i:rank * i + 8, mine]
-            part[nb + b + i] = pin[rank * i + 8:rank * i + 16, mine]
-            part[2 * nb + b + i] = pback[rank * i:rank * i + 8, mine]
-            part[3 * nb + b + i] = pback[rank * i + 8:rank * i + 16, mine]
-
-    sums = []
-    for k in (8, 7, 9, 6, 10, 5, 11, 4, 12, 3, 13, 2, 14, 1, 15):
-        tt = lax.rem(t + k, NT)
-        sums.append(copy_to(part.at[tt], part_in.at[k], (r, tt)))
-
     ag_step(3)
+    rank_middle(1)
+    rback = rank_end(0)
+    going_a = grads_start(rback, tok, gxa, owna)
     rs_hop(1, False)
     ag_mate[0].wait_recv()
     tgrad[...] = dot_nt(cotf[y], w[:, pl.ds(pl.multiple_of(y * 256, 256), 256)])
     through_steps((1, 1))
-
-    total = part[t]
-    for made in sums:
-        made.wait_recv()
-    for k in range(1, NT):
-        total = total + part_in[k]
-    full[t] = total
-    spread = []
-    for k in (8, 7, 9, 6, 10, 5, 11, 4, 12, 3, 13, 2, 14, 1, 15):
-        spread.append(copy_to(full.at[t], full.at[t], (r, lax.rem(t + k, NT))))
-
+    rin = rank_end(1)
+    going_b = grads_start(rin, cot, gxb, ownb)
     rs_hop(1, True)
     ag_right[4].wait_recv()
     ag_left[4].wait_recv()
     far = cot_at(lax.rem(y + 4, NY), c, 0, rows)
     ag_mate.append(copy_to(far, far, mate))
-    through_steps((2, -1), (3, 2), (4, -2))
-
-    for made in spread:
-        made.wait_recv()
-    rin = [two_parts(jnp.concatenate([full[b], full[nb + b]], axis=0)) for b in range(nb)]
-    rback = [two_parts(jnp.concatenate([full[2 * nb + b], full[3 * nb + b]], axis=0)) for b in range(nb)]
+    going_a = grads_middle(going_a, gxa, owna, za_out, za_in, 0)
+    through_steps((2, -1))
+    going_b = grads_middle(going_b, gxb, ownb, zb_out, zb_in, feat)
     for b in range(nb):
-        here = pl.ds(b * BLOCK, BLOCK)
-        da = dot(rback[b], tok[here, :])
-        db = dot(rin[b], cot[here, :])
-        own = jnp.concatenate([da[:rank] + da[rank:], db[:rank] + db[rank:]], axis=1)
-        gown[b] = own
-        gx[0, b] = encode_grads(own, feat)
-    grads_x = [copy_to(gx.at[0], gx.at[k], at_x(k)) for k in (2, 1, 3)]
-
-    for b in range(nb):
-        here = pl.ds(b * BLOCK, BLOCK)
-        amap = jnp.concatenate([chosen[b][:, :feat]] * 2, axis=0)
-        bmap = jnp.concatenate([chosen[b][:, feat:]] * 2, axis=0)
-        tgrad[here, :] += 2.0 * dot_tn(rback[b], amap)
-        base[0, here, :] += 2.0 * dot_tn(rin[b], bmap)
-    through_steps((5, 3), (6, -3))
-
-    for made in grads_x:
-        made.wait_recv()
-    for k in range(1, NX):
-        for b in range(nb):
-            one, two = decode_grads(gx[k, b], feat)
-            gown[k * nb + b, :, :feat] = one
-            gown[k * nb + b, :, feat:] = two
-    grads_z = {}
-    for d in (4, 3, 5, 2, 6, 1, 7, 0):
-        owner = lax.rem(z + d, NZ) * NX + x
-        acc = jnp.zeros((rank, grouped), F32)
-        for k in range(NX):
-            weight = jnp.sum(jnp.where(lane == owner, sel[k], 0.0), axis=1, keepdims=True)
-            for b in range(nb):
-                acc = acc + weight[b:b + 1, :] * gown[k * nb + b]
-        if d:
-            gz_out[d] = encode_grads(acc, feat)
-            grads_z[d] = copy_to(gz_out.at[d], gz_in.at[d], at_z(d))
-        else:
-            gtotal[...] = acc
-
-    through_steps((7, 4))
-    out_tg = pltpu.make_async_copy(tgrad, tgrad_out, lsem.at[0])
-    out_tg.start()
-
+        here = blocks_of(b)
+        tgrad[here, :] += 2.0 * dot_tn(rback[b], jnp.concatenate([chosen_a[b]] * 2, axis=0))
+        base[0, here, :] += 2.0 * dot_tn(rin[b], jnp.concatenate([chosen_b[b]] * 2, axis=0))
     rs_take(1, "B", 1)
     rs_take(-1, "A", 1)
     rs_take(1, "A", 1)
     rs_take(-1, "B", 1)
     out_pj = pltpu.make_async_copy(base.at[0], proj, lsem.at[1])
     out_pj.start()
+    through_steps((3, 2), (4, -2), (5, 3), (6, -3), (7, 4))
+    out_tg = pltpu.make_async_copy(tgrad, tgrad_out, lsem.at[0])
+    out_tg.start()
 
     for made in counted:
         made.wait_recv()
-    blocks_of = jnp.sum(cnt[...], axis=0)
-    mine = jnp.sum(jnp.where(lane == r, blocks_of, 0.0), axis=1, keepdims=True)
+    all_counts = jnp.sum(cnt[...], axis=0)
+    mine = jnp.sum(jnp.where(lane == r, all_counts, 0.0), axis=1, keepdims=True)
     scale = 2.0 / jnp.maximum(mine * float(BLOCK), 1.0)
-    acc_in, acc_out = gtotal[:, :feat], gtotal[:, feat:]
-    for d in (1, 7, 2, 6, 3, 5, 4):
-        grads_z[d].wait_recv()
-        one, two = decode_grads(gz_in[d], feat)
-        acc_in, acc_out = acc_in + one, acc_out + two
-    gtotal[:, :feat] = acc_in * scale
-    gtotal[:, feat:] = acc_out * scale
+    grads_end(going_a, za_in, 0, feat, scale)
+    grads_end(going_b, zb_in, feat, grouped - feat, scale)
     out_gi = pltpu.make_async_copy(gtotal.at[:, pl.ds(0, feat)], gin.at[0], lsem.at[2])
     out_go = pltpu.make_async_copy(gtotal.at[:, pl.ds(feat, grouped - feat)], gout.at[0], lsem.at[3])
     out_gi.start()
@@ -384,7 +404,7 @@
         made.wait()
 
 
-COPIES = 128
+COPIES = 224
 
 
 def shards(tok, w, cot, ain, aout, tenant, storage):
@@ -407,7 +427,8 @@
             pltpu.VMEM((rows, cols), BF16),
             pltpu.VMEM((rows, feat), F32),
             pltpu.VMEM((rank, grouped), F32),
-            pltpu.VMEM((NX * NZ, rank, grouped), BF16),
+            pltpu.VMEM((NX * NZ, rank, feat), BF16),
+            pltpu.VMEM((NX * NZ, rank, cols), BF16),
             pltpu.VMEM((NX, nb, 128), F32),
             pltpu.VMEM((NZ, 1, 128), F32),
             pltpu.VMEM((NY, rows, NC * cols), BF16),
@@ -417,13 +438,17 @@
             pltpu.VMEM((14, rows // 2 + 16, cols), BF16),
             pltpu.VMEM((7, rows // 2 + 16, cols), BF16),
             pltpu.VMEM((7, rows // 2 + 16, cols), BF16),
-            pltpu.VMEM((NT, 8, 128), F32),
-            pltpu.VMEM((NT, 8, 128), F32),
-            pltpu.VMEM((NT, 8, 128), F32),
-            pltpu.VMEM((NX, nb, rank, grouped + 128), BF16),
-            pltpu.VMEM((NX * nb, rank, grouped), F32),
-            pltpu.VMEM((NZ, rank, grouped + 128), BF16),
-            pltpu.VMEM((NZ, rank, grouped + 128), BF16),
+            pltpu.VMEM((2, NT, 4, 128), F32),
+            pltpu.VMEM((2, NT, 4, 128), F32),
+            pltpu.VMEM((2, NT, 4, 128), F32),
+            pltpu.VMEM((NX, nb, rank, feat + 128), BF16),
+            pltpu.VMEM((NX, nb, rank, cols + 128), BF16),
+            pltpu.VMEM((NX * nb, rank, feat), F32),
+            pltpu.VMEM((NX * nb, rank, cols), F32),
+            pltpu.VMEM((NZ, rank, feat + 128), BF16),
+            pltpu.VMEM((NZ, rank, cols + 128), BF16),
+            pltpu.VMEM((NZ, rank, feat + 128), BF16),
+            pltpu.VMEM((NZ, rank, cols + 128), BF16),
             pltpu.SemaphoreType.DMA((COPIES,)),
             pltpu.SemaphoreType.DMA((COPIES,)),
             pltpu.SemaphoreType.DMA((6,)),

time: 64.1 us -> 59.1 us (0.922)
  Pallas kernels: 63.2 us -> 58.2 us
    pallas_call x1, Pallas kernels: 60.9 us -> 55.9 us  [shards(): pl.pallas_call(kernel, out_shape=tuple((jax.ShapeDtypeStruct(shape, F32)...]
where the time goes in v4:
time: 59.1 us; the launch traced here: 58.9 us
  Pallas kernels  58.2 us (98%)
  between operations  0.64 us (1%)
    pallas_call x1, Pallas kernels, shards(): pl.pallas_call(kernel, out_shape=tuple((jax.ShapeDtypeStruct(shape, F32)...  55.9 us
    pallas_call x1, Pallas kernels, shards(): pl.pallas_call(finish, out_shape=tuple((jax.ShapeDtypeStruct(shape, F32)...  2.36 us

profile of v4, /device:TPU:1, one launch (start us, length us, event | category | flops | bytes accessed | tf_op | source)
XLA Modules:
  0.0 58.9 jit_solution(3458409993916292196)
XLA Ops:
  0.6 55.9 %shard_map.102 = (f32[512,128]{1,0:T(8,128)}, f32[512,512]{1,0:T(8,128)}, f32[1,16,512]{2,1,0:T(8,128)}, f32[1,16,128]{2,1,0:T(8,128)}) custom-call(s32[4]{0:T(128)} %tenant.1, s32[32]{0:T(128)} %storage.1, bf16[512,512]{1,0:T(8,128)(2,1)} %tok_in.1, bf16[512,2048]{1,0:T(8,128)(2,1)} %w_in.1, bf16[512,128]{1,0:T(8,128)(2,1)} %cot_in.1, ...), custom_call_target="tpu_custom_call" | custom-call | tf_op jit(solution)/shard_map/pallas_call | solution.py:419
  56.5 2.4 %shard_map.103 = (f32[512,128]{1,0:T(8,128)}, f32[512,512]{1,0:T(8,128)}, f32[1,16,512]{2,1,0:T(8,128)}, f32[1,16,128]{2,1,0:T(8,128)}) custom-call(f32[512,128]{1,0:T(8,128)} %get-tuple-element.8.refs_0_, f32[512,512]{1,0:T(8,128)} %get-tuple-element.9.refs_1_, f32[1,16,512]{2,1,0:T(8,128)} %get-tuple-element.10.refs_2_, ...), custom_call_target="tpu_custom_call" | custom-call | tf_op jit(solution)/shard_map/pallas_call | solution.py:460

commit v5 on v4

--- a/solution.py
+++ b/solution.py
@@ -134,31 +134,29 @@
         yy = lax.rem(y + d, NY)
         return pl.ds(pl.multiple_of(yy * (NC * 128) + cc * 128, 128), 128)
 
-    for made in local[:4]:
-        made.wait()
     pl.semaphore_wait(barrier, len(greeted))
 
     near_z, near_x = (1, 7, 2, 6, 3, 5, 4), (2, 1, 3)
     along_z, along_x = {}, {}
-    for kind, maps in (("b", maps_b), ("a", maps_a)):
+    for kind, own, maps in (("b", aout, maps_b), ("a", ain, maps_a)):
         for k in near_z:
-            along_z[kind, k] = copy_to(maps.at[r], maps.at[r], at_z(k))
-        along_x[kind] = [copy_to(maps.at[r], maps.at[r], at_x(k)) for k in near_x]
+            along_z[kind, k] = copy_to(own.at[0], maps.at[r], at_z(k))
+        along_x[kind] = [copy_to(own.at[0], maps.at[r], at_x(k)) for k in near_x]
 
     def cot_at(yy, cc, lo, size):
         return cotf.at[yy, pl.ds(lo, size), pl.ds(pl.multiple_of(cc * 128, 128), 128)]
 
     ag_right, ag_left, ag_mate = {}, {}, []
-    ag_right[1] = copy_to(cot, cot_at(y, c, 0, rows), at_y(1))
-    ag_left[1] = copy_to(cot, cot_at(y, c, 0, rows), at_y(-1))
-    for made in local[4:]:
+    ag_right[1] = copy_to(cot_in, cot_at(y, c, 0, rows), at_y(1))
+    ag_left[1] = copy_to(cot_in, cot_at(y, c, 0, rows), at_y(-1))
+    for made in local:
         made.wait()
     tok_mate = copy_to(tok, tokp, mate)
     w_mate = {}
 
     for d in (4, 3, 5, 2, 6, 1, 7, 0):
         w_mate[d] = copy_to(w.at[:, w_cols(d, other)], wp.at[d], mate)
-    ag_mate.append(copy_to(cot, cot_at(y, c, 0, rows), mate))
+    ag_mate.append(copy_to(cot_in, cot_at(y, c, 0, rows), mate))
     sel_x = [copy_to(sel.at[0], sel.at[k], at_x(k)) for k in (1, 2, 3)]
 
     def mate_pair(pair):
@@ -229,7 +227,17 @@
             gx[0, b] = encode_wide(g)
         return [copy_to(gx.at[0], gx.at[k], at_x(k)) for k in near_x]
 
-    def grads_middle(going, gx, own, out, into, lo):
+    far_z = (4, 3, 5, 2, 6, 1, 7)
+
+    def owner_weights():
+        return {
+            (d, k): jnp.sum(
+                jnp.where(lane == lax.rem(z + d, NZ) * NX + x, sel[k], 0.0), axis=1, keepdims=True
+            )
+            for d in range(NZ) for k in range(NX)
+        }
+
+    def grads_middle(weights, going, gx, own, out, into, lo):
         for made in going:
             made.wait_recv()
         for k in range(1, NX):
@@ -237,13 +245,11 @@
                 own[k * nb + b] = decode_wide(gx[k, b])
         made = {}
         n = own.shape[2]
-        for d in near_z + (0,):
-            owner = lax.rem(z + d, NZ) * NX + x
+        for d in far_z + (0,):
             acc = jnp.zeros((rank, n), F32)
             for k in range(NX):
-                weight = jnp.sum(jnp.where(lane == owner, sel[k], 0.0), axis=1, keepdims=True)
                 for b in range(nb):
-                    acc = acc + weight[b:b + 1, :] * own[k * nb + b]
+                    acc = acc + weights[d, k][b:b + 1, :] * own[k * nb + b]
             if d:
                 out[d] = encode_wide(acc)
                 made[d] = copy_to(out.at[d], into.at[d], at_z(d))
@@ -312,30 +318,30 @@
     own_pair(pairs[0])
     maps_on("b", 2, 6)
     maps_on("a", 1, 7)
-    own_pair(pairs[1])
     tok_mate.wait_recv()
     mate_pair(pairs[0])
     rs_send(1, "A", 4)
     rs_send(-1, "B", 4)
     maps_on("b", 3, 5)
     maps_on("a", 2, 6)
+    ag_step(1)
     maps_on("b", 4)
     rs_send(1, "B", 3)
+    own_pair(pairs[1])
     mate_pair(pairs[1])
     rs_send(-1, "A", 3)
-    ag_step(1)
     maps_on("a", 3, 5)
     maps_on("a", 4)
     chosen_b = rank_start(0, "b", maps_b, cot)
+    rs_hop(3, True)
     own_pair(pairs[2])
+    ag_step(2)
+    mate_pair(pairs[2])
     own_pair(pairs[3])
-    mate_pair(pairs[2])
-    rs_hop(3, True)
-    ag_step(2)
     chosen_a = rank_start(1, "a", maps_a, tok)
     rank_middle(0)
+    rs_hop(2, False)
     mate_pair(pairs[3])
-    rs_hop(2, False)
     for made in sel_x:
         made.wait_recv()
     cnt[0] = jnp.sum(jnp.sum(sel[...], axis=0), axis=0, keepdims=True)
@@ -346,19 +352,19 @@
     rback = rank_end(0)
     going_a = grads_start(rback, tok, gxa, owna)
     rs_hop(1, False)
-    ag_mate[0].wait_recv()
-    tgrad[...] = dot_nt(cotf[y], w[:, pl.ds(pl.multiple_of(y * 256, 256), 256)])
-    through_steps((1, 1))
-    rin = rank_end(1)
-    going_b = grads_start(rin, cot, gxb, ownb)
     rs_hop(1, True)
     ag_right[4].wait_recv()
     ag_left[4].wait_recv()
     far = cot_at(lax.rem(y + 4, NY), c, 0, rows)
     ag_mate.append(copy_to(far, far, mate))
-    going_a = grads_middle(going_a, gxa, owna, za_out, za_in, 0)
-    through_steps((2, -1))
-    going_b = grads_middle(going_b, gxb, ownb, zb_out, zb_in, feat)
+    weights = owner_weights()
+    ag_mate[0].wait_recv()
+    tgrad[...] = dot_nt(cotf[y], w[:, pl.ds(pl.multiple_of(y * 256, 256), 256)])
+    rin = rank_end(1)
+    going_b = grads_start(rin, cot, gxb, ownb)
+    going_a = grads_middle(weights, going_a, gxa, owna, za_out, za_in, 0)
+    going_b = grads_middle(weights, going_b, gxb, ownb, zb_out, zb_in, feat)
+    through_steps((1, 1), (2, -1))
     for b in range(nb):
         here = blocks_of(b)
         tgrad[here, :] += 2.0 * dot_tn(rback[b], jnp.concatenate([chosen_a[b]] * 2, axis=0))

time: 59.1 us -> 58.2 us (0.985)
  Pallas kernels: 58.2 us -> 57.4 us
    pallas_call x1, Pallas kernels: 55.9 us -> 55.1 us  [shards(): pl.pallas_call(kernel, out_shape=tuple((jax.ShapeDtypeStruct(shape, F32)...]
where the time goes in v5:
time: 58.2 us; the launch traced here: 58.1 us
  Pallas kernels  57.4 us (99%)
  between operations  0.64 us (1%)
    pallas_call x1, Pallas kernels, shards(): pl.pallas_call(kernel, out_shape=tuple((jax.ShapeDtypeStruct(shape, F32)...  55.1 us
    pallas_call x1, Pallas kernels, shards(): pl.pallas_call(finish, out_shape=tuple((jax.ShapeDtypeStruct(shape, F32)...  2.36 us

profile of v5, /device:TPU:1, one launch (start us, length us, event | category | flops | bytes accessed | tf_op | source)
XLA Modules:
  0.0 58.1 jit_solution(17096789819006941019)
XLA Ops:
  0.6 55.1 %shard_map.102 = (f32[512,128]{1,0:T(8,128)}, f32[512,512]{1,0:T(8,128)}, f32[1,16,512]{2,1,0:T(8,128)}, f32[1,16,128]{2,1,0:T(8,128)}) custom-call(s32[4]{0:T(128)} %tenant.1, s32[32]{0:T(128)} %storage.1, bf16[512,512]{1,0:T(8,128)(2,1)} %tok_in.1, bf16[512,2048]{1,0:T(8,128)(2,1)} %w_in.1, bf16[512,128]{1,0:T(8,128)(2,1)} %cot_in.1, ...), custom_call_target="tpu_custom_call" | custom-call | tf_op jit(solution)/shard_map/pallas_call | solution.py:425
  55.7 2.4 %shard_map.103 = (f32[512,128]{1,0:T(8,128)}, f32[512,512]{1,0:T(8,128)}, f32[1,16,512]{2,1,0:T(8,128)}, f32[1,16,128]{2,1,0:T(8,128)}) custom-call(f32[512,128]{1,0:T(8,128)} %get-tuple-element.8.refs_0_, f32[512,512]{1,0:T(8,128)} %get-tuple-element.9.refs_1_, f32[1,16,512]{2,1,0:T(8,128)} %get-tuple-element.10.refs_2_, ...), custom_call_target="tpu_custom_call" | custom-call | tf_op jit(solution)/shard_map/pallas_call | solution.py:466
